TPU v7x, 32 devices: a whole 2x2x4 slice. The times are simulated.
32 devices in a mesh: gx: 8 (over y, x, core), gy: 4 (over z).
Axes of the slice: x: 2, y: 2, z: 4, core: 2. Of those that a mesh axis runs over, the one named last changes fastest.
Arguments:
- fields: bfloat16 [128, 128, 256], P('gx', 'gy'), may hold values from -6 to 6
- w_down: bfloat16 [3, 3, 3, 32, 32], replicated, may hold values from -0.21875 to 0.21875
- w_pool: bfloat16 [2, 2, 2, 32, 64], replicated, may hold values from -0.375 to 0.375
- w_mid: bfloat16 [3, 3, 3, 64, 64], replicated, may hold values from -0.15625 to 0.15625
- w_unpool: bfloat16 [2, 2, 2, 64, 32], replicated, may hold values from -0.75 to 0.75
- w_up: bfloat16 [3, 3, 3, 32, 32], replicated, may hold values from -0.21875 to 0.21875
- cotangent: bfloat16 [128, 128, 256], P('gx', 'gy'), may hold values from -6 to 6
Outputs:
- output: bfloat16 [128, 128, 256], P('gx', 'gy')
- grad_fields: bfloat16 [128, 128, 256], P('gx', 'gy')
- grad_down: float32 [3, 3, 3, 32, 32], replicated
- grad_pool: float32 [2, 2, 2, 32, 64], replicated
- grad_mid: float32 [3, 3, 3, 64, 64], replicated
- grad_unpool: float32 [2, 2, 2, 64, 32], replicated
- grad_up: float32 [3, 3, 3, 32, 32], replicated
All inputs are finite; a program needn't handle non-finite values.
Results may differ from a plain program's by a relative error of at most 0.0071.
Values may be sent and summed in bfloat16 or wider, within the bound.
A program may use at most 128 MiB of HBM per device.

v0:
```python
import math

import jax
import jax.numpy as jnp
from jax import lax
from jax.sharding import PartitionSpec as P


def padded_2(block, sides, width):
    for axis, dim in sides:
        count = lax.axis_size(axis)
        forward = [(i, i + 1) for i in range(count - 1)]
        forward.append((count - 1, 0))
        backward = [(target, source) for source, target in forward]
        low = lax.ppermute(
            lax.slice_in_dim(block, block.shape[dim] - width, None, axis=dim), axis, forward
        )
        high = lax.ppermute(lax.slice_in_dim(block, 0, width, axis=dim), axis, backward)
        block = jnp.concatenate([low, block, high], axis=dim)
    return block


def dsilu(value):
    sig = jax.nn.sigmoid(value)
    return sig * (1.0 + value * (1.0 - sig))


def plane_shifts(planes):
    return jnp.stack([jnp.eye(planes, k=1 - kk, dtype=jnp.float32) for kk in range(3)])


def widened(weight, copies):
    cout = weight.shape[-1]
    tiled = jnp.tile(jnp.eye(cout, dtype=weight.dtype), (1, copies))
    wide = jnp.dot(weight.reshape(-1, cout), tiled, preferred_element_type=jnp.float32)
    return wide.astype(jnp.bfloat16).reshape(weight.shape[:-1] + (copies * cout,))


def lane_offset(planes, cout):
    lanes = lax.broadcasted_iota(jnp.int32, (planes, 1, planes * cout), 2) // cout
    return lanes - lax.broadcasted_iota(jnp.int32, (planes, 1, planes * cout), 0)


def band_matrix(weight, planes):
    cin, cout = weight.shape[3], weight.shape[4]
    wide = widened(weight, planes)
    offset = lane_offset(planes, cout)
    band = jnp.zeros((3, 3, planes, cin, planes * cout), jnp.bfloat16)
    for kk in range(3):
        band = jnp.where(offset == 1 - kk, wide[:, :, kk][:, :, None], band)
    return band.reshape(9 * planes * cin, planes * cout)


def band_to_weight(dband, planes, cin, cout):
    shifts = plane_shifts(planes)
    return jnp.einsum("kpz,abpczo->abkco", shifts, dband.reshape(3, 3, planes, cin, planes, cout))


def flipped(weight):
    return jnp.transpose(weight[::-1, ::-1, ::-1], (0, 1, 2, 4, 3))


def fine_rim(field):
    return padded_2(field, (("gx", 0), ("gy", 1)), 1)


def coarse_rim(field):
    return padded_2(field, (("gx", 0), ("gy", 1)), 1)


def columns(padded):
    xs = padded.shape[0] - 2
    ys = padded.shape[1] - 2
    cols = jnp.concatenate(
        [padded[aa : aa + xs, bb : bb + ys, :] for aa in range(3) for bb in range(3)], axis=2
    )
    return cols.reshape(xs * ys, -1)


def conv_padded(padded, band):
    xs = padded.shape[0] - 2
    ys = padded.shape[1] - 2
    return jnp.dot(columns(padded), band, preferred_element_type=jnp.float32).reshape(xs, ys, -1)


def weight_grad(padded, dout, planes, cin, cout):
    flat = dout.reshape(-1, dout.shape[2])
    dband = lax.dot_general(
        columns(padded), flat, (((0,), (0,)), ((), ())), preferred_element_type=jnp.float32
    )
    return band_to_weight(dband, planes, cin, cout)


def split_fine(field):
    xs, ys, width = field.shape
    parts = field.reshape(xs // 2, 2, ys // 2, 2, width).transpose(0, 2, 1, 3, 4)
    return parts.reshape(xs // 2 * (ys // 2), 4 * width)


def merge_fine(flat, xs, ys):
    width = flat.shape[1] // 4
    return (
        flat.reshape(xs // 2, ys // 2, 2, 2, width).transpose(0, 2, 1, 3, 4).reshape(xs, ys, width)
    )


def pool_matrix(weight, half):
    cout = weight.shape[4]
    wide = widened(weight, half)
    offset = lane_offset(half, cout)[:, None]
    mat = jnp.where(offset == 0, wide[:, :, None], jnp.zeros((), jnp.bfloat16))
    return mat.reshape(-1, half * cout)


def summed_over(parts, axes, scale):
    count = 1
    for axis in axes:
        count *= lax.axis_size(axis)
    flat = jnp.concatenate([part.reshape(-1, 128) for part in parts], axis=0)
    rows = -(-flat.shape[0] // (8 * count)) * 8
    flat = jnp.pad(flat, ((0, rows * count - flat.shape[0]), (0, 0)))
    pieces = lax.all_to_all(flat.reshape(count, rows, 128), axes, 0, 0, tiled=True)
    whole = lax.all_gather(jnp.sum(pieces, axis=0) * scale, axes, axis=0, tiled=True)
    out, start = [], 0
    for part in parts:
        size = part.size // 128
        out.append(whole[start : start + size].reshape(part.shape))
        start += size
    return tuple(out)


def per_device(fields, w_down, w_pool, w_mid, w_unpool, w_up, cotangent):
    cf = w_down.shape[3]
    cc = w_mid.shape[3]
    xs, ys = (fields.shape[0], fields.shape[1])
    width = fields.shape[2]
    planes = width // cf
    half = planes // 2
    pmat = pool_matrix(w_pool, half)
    umat_t = pool_matrix(jnp.swapaxes(w_unpool, 3, 4), half)
    joined = padded_2(jnp.concatenate((fields, cotangent), axis=2), (("gx", 0), ("gy", 1)), 1)
    fields_pad = joined[:, :, :width]
    cot_pad = joined[:, :, width:]
    pre_down = conv_padded(fields_pad, band_matrix(w_down, planes))
    hidden = jax.nn.silu(pre_down).astype(jnp.bfloat16)
    hidden_parts = split_fine(hidden)
    pre_pool = jnp.dot(hidden_parts, pmat, preferred_element_type=jnp.float32).reshape(
        xs // 2, ys // 2, -1
    )
    coarse = jax.nn.silu(pre_pool).astype(jnp.bfloat16)
    coarse_pad = coarse_rim(coarse)
    pre_mid = conv_padded(coarse_pad, band_matrix(w_mid, half))
    middle = (coarse.astype(jnp.float32) + jax.nn.silu(pre_mid)).astype(jnp.bfloat16)
    middle_flat = middle.reshape(-1, middle.shape[2])
    lifted = lax.dot_general(
        middle_flat, umat_t, (((1,), (1,)), ((), ())), preferred_element_type=jnp.float32
    )
    pre_up = hidden.astype(jnp.float32) + merge_fine(lifted, xs, ys)
    skip = jax.nn.silu(pre_up).astype(jnp.bfloat16)
    skip_pad = fine_rim(skip)
    output = (fields.astype(jnp.float32) + conv_padded(skip_pad, band_matrix(w_up, planes))).astype(
        jnp.bfloat16
    )
    d_up = (conv_padded(cot_pad, band_matrix(flipped(w_up), planes)) * dsilu(pre_up)).astype(
        jnp.bfloat16
    )
    d_up_parts = split_fine(d_up)
    d_middle = jnp.dot(d_up_parts, umat_t, preferred_element_type=jnp.float32)
    d_middle = d_middle.reshape(xs // 2, ys // 2, -1)
    d_mid = (d_middle * dsilu(pre_mid)).astype(jnp.bfloat16)
    d_coarse = d_middle + conv_padded(coarse_rim(d_mid), band_matrix(flipped(w_mid), half))
    d_pool = (d_coarse * dsilu(pre_pool)).astype(jnp.bfloat16)
    d_pool_flat = d_pool.reshape(-1, d_pool.shape[2])
    back = lax.dot_general(
        d_pool_flat, pmat, (((1,), (1,)), ((), ())), preferred_element_type=jnp.float32
    )
    d_hidden = d_up.astype(jnp.float32) + merge_fine(back, xs, ys)
    d_down = (d_hidden * dsilu(pre_down)).astype(jnp.bfloat16)
    grad_fields = (
        cotangent.astype(jnp.float32)
        + conv_padded(fine_rim(d_down), band_matrix(flipped(w_down), planes))
    ).astype(jnp.bfloat16)
    part_up = weight_grad(skip_pad, cotangent, planes, cf, cf)
    part_mid = weight_grad(coarse_pad, d_mid, half, cc, cc)
    part_down = weight_grad(fields_pad, d_down, planes, cf, cf)
    eye = jnp.eye(half, dtype=jnp.float32)
    d_umat = lax.dot_general(
        middle_flat, d_up_parts, (((0,), (0,)), ((), ())), preferred_element_type=jnp.float32
    )
    part_unpool = jnp.einsum("yz,yoijzlf->ijlof", eye, d_umat.reshape(half, cc, 2, 2, half, 2, cf))
    d_pmat = lax.dot_general(
        hidden_parts, d_pool_flat, (((0,), (0,)), ((), ())), preferred_element_type=jnp.float32
    )
    part_pool = jnp.einsum("yz,ijylczo->ijlco", eye, d_pmat.reshape(2, 2, half, 2, cf, half, cc))
    scale = 1.0 / math.sqrt(xs * ys * planes * lax.axis_size("gx") * lax.axis_size("gy"))
    grad_down, grad_pool, grad_mid, grad_unpool, grad_up = summed_over(
        (part_down, part_pool, part_mid, part_unpool, part_up), ("gx", "gy"), scale
    )
    return (output, grad_fields, grad_down, grad_pool, grad_mid, grad_unpool, grad_up)


def solution(mesh):
    placed = (P("gx", "gy", None), P(), P(), P(), P(), P(), P("gx", "gy", None))
    return jax.shard_map(
        per_device,
        mesh=mesh,
        in_specs=placed,
        out_specs=(P("gx", "gy", None), P("gx", "gy", None), P(), P(), P(), P(), P()),
        check_vma=False,
    )
```

profile of v0, /device:TPU:0, one launch (start us, length us, event | category | flops | bytes accessed | tf_op | source)
XLA Modules:
  0.0 229.6 jit_solution(13724199050406112962)
XLA Ops:
  3.8 2.9 %collective-permute-start.1 = (bf16[1,32,512]{2,1,0:T(8,128)(2,1)}, bf16[1,32,512]{2,1,0:T(8,128)(2,1)}, u32[]{:S(2)}, u32[]{:S(2)}) collective-permute-start(bf16[1,32,512]{2,1,0:T(8,128)(2,1)} %get-tuple-element.52), channel_id=1, source_target_pairs={{4,0},{8,4},{12,8},{16,12},{20,16},{24,20},{28,24},{0,28},{5,1},{9... | collective-permute-start | bytes 98312 | tf_op jit(solution)/shard_map/ppermute | solution.py:18
  14.8 1.7 convolution_convert_fusion.6
  23.1 1.6 select_select_fusion.1
  24.7 2.1 select_select_fusion
  28.4 2.4 %collective-permute-start.2 = (bf16[18,1,512]{2,1,0:T(2,128)(2,1)S(1)}, bf16[18,1,512]{2,1,0:T(2,128)(2,1)S(1)}, u32[]{:S(2)}, u32[]{:S(2)}) collective-permute-start(bf16[18,1,512]{2,1,0:T(2,128)(2,1)S(1)} %get-tuple-element.46), channel_id=1, source_target_pairs={{0,1},{1,2},{2,3},{3,0},{4,5},{5,6},{6,7},{7,4},{8,9},{9,10},{10,1... | collective-permute-start | bytes 55304 | tf_op jit(solution)/shard_map/ppermute | solution.py:15
  30.7 2.1 collective-permute-start.3
  32.8 2.1 collective-permute-done.2
  40.2 1.6 multiply_convert_fusion.2
  43.0 1.9 multiply_convert_fusion.4
  45.0 2.6 %collective-permute-start.5 = (bf16[1,16,256]{2,1,0:T(8,128)(2,1)S(1)}, bf16[1,16,256]{2,1,0:T(8,128)(2,1)S(1)}, u32[]{:S(2)}, u32[]{:S(2)}) collective-permute-start(bf16[1,16,256]{2,1,0:T(8,128)(2,1)S(1)} %get-tuple-element.90), channel_id=1, source_target_pairs={{4,0},{8,4},{12,8},{16,12},{20,16},{24,20},{28,24},{0,28},{5,1},{9... | collective-permute-start | bytes 24584 | tf_op jit(solution)/shard_map/ppermute | solution.py:18
  50.8 2.7 %collective-permute-start.7 = (bf16[10,1,256]{2,1,0:T(2,128)(2,1)S(1)}, bf16[10,1,256]{2,1,0:T(2,128)(2,1)S(1)}, u32[]{:S(2)}, u32[]{:S(2)}) collective-permute-start(bf16[10,1,256]{2,1,0:T(2,128)(2,1)S(1)} %get-tuple-element.83), channel_id=1, source_target_pairs={{1,0},{2,1},{3,2},{0,3},{5,4},{6,5},{7,6},{4,7},{9,8},{10,9},{11,1... | collective-permute-start | bytes 15368 | tf_op jit(solution)/shard_map/ppermute | solution.py:18
  56.3 2.4 %copy.46 = bf16[512,2304]{0,1:T(8,128)(2,1)} copy(bf16[512,2304]{1,0:T(8,128)(2,1)S(1)} %bitcast.299) | data formatting | bytes 4718592 | tf_op jit(solution)/shard_map/reshape | solution.py:77
  59.0 2.5 %add_convert_fusion = (bf16[8,16,256]{2,1,0:T(8,128)(2,1)S(1)}, f32[8,16,256]{2,1,0:T(8,128)}) fusion(bf16[8,16,256]{2,1,0:T(8,128)(2,1)S(1)} %get-tuple-element.107, bf16[8,16,2304]{2,1,0:T(8,128)(2,1)S(1)} %constant_dynamic-update-slice_fusion.3, bf16[2304,256,1]{1,0,2:T(8,128)(2,1)} %bitcast.322), kind=kOutput, calls=%fused_computation.118 | convolution fusion | flops 151224320 | bytes 2031616 | tf_op jit(solution)/shard_map/dot_general | solution.py:83
  62.6 2.4 %fusion.20 = bf16[16,32,256]{2,1,0:T(8,128)(2,1)S(1)} fusion(bf16[16,32,2304]{2,1,0:T(8,128)(2,1)} %copy-done.23, bf16[2304,256,1]{1,0,2:T(8,128)(2,1)S(1)} %bitcast.323, f32[16,32,256]{2,1,0:T(8,128)S(1)} %reshape.671, bf16[16,32,256]{2,1,0:T(8,128)(2,1)S(1)} %copy-done.15), kind=kOutput, calls=%fused_computation.25 | convolution fusion | flops 605421568 | bytes 4587520 | tf_op jit(solution)/shard_map/dot_general | solution.py:83
  68.3 2.6 %collective-permute-start.13 = (bf16[1,16,256]{2,1,0:T(8,128)(2,1)S(1)}, bf16[1,16,256]{2,1,0:T(8,128)(2,1)S(1)}, u32[]{:S(2)}, u32[]{:S(2)}) collective-permute-start(bf16[1,16,256]{2,1,0:T(8,128)(2,1)S(1)} %get-tuple-element.86), channel_id=1, source_target_pairs={{4,0},{8,4},{12,8},{16,12},{20,16},{24,20},{28,24},{0,28},{5,1},{9... | collective-permute-start | bytes 24584 | tf_op jit(solution)/shard_map/ppermute | solution.py:18
  73.3 2.4 %fusion.10 = f32[3,3,3,64,64]{4,2,3,1,0:T(4,128)S(1)} fusion(bf16[3,3,4,64,4,64]{5,3,4,2,1,0:T(8,128)(2,1)S(1)} %fusion.60, pred[1,4,4]{2,0,1:T(4,128)(4,1)S(1)} %get-tuple-element.130, pred[1,4,4]{2,0,1:T(4,128)(4,1)S(1)} %copy-done.34, pred[1,4,4]{2,0,1:T(4,128)(4,1)S(1)} %iota_compare_fusion.7), kind=kOutput, calls=%fused_computation.12 | convolution fusion | flops 3539040 | bytes 1622064 | tf_op jit(solution)/shard_map/kpz,abpczo->abkco/dot_general | solution.py:56
  76.1 3.8 %collective-permute-start.15 = (bf16[10,1,256]{2,1,0:T(2,128)(2,1)S(1)}, bf16[10,1,256]{2,1,0:T(2,128)(2,1)S(1)}, u32[]{:S(2)}, u32[]{:S(2)}) collective-permute-start(bf16[10,1,256]{2,1,0:T(2,128)(2,1)S(1)} %get-tuple-element.79), channel_id=1, source_target_pairs={{1,0},{2,1},{3,2},{0,3},{5,4},{6,5},{7,6},{4,7},{9,8},{10,9},{11,1... | collective-permute-start | bytes 15368 | tf_op jit(solution)/shard_map/ppermute | solution.py:18
  81.8 2.6 %collective-permute-start.9 = (bf16[1,32,256]{2,1,0:T(8,128)(2,1)}, bf16[1,32,256]{2,1,0:T(8,128)(2,1)S(1)}, u32[]{:S(2)}, u32[]{:S(2)}) collective-permute-start(bf16[1,32,256]{2,1,0:T(8,128)(2,1)} %get-tuple-element.76), channel_id=1, source_target_pairs={{4,0},{8,4},{12,8},{16,12},{20,16},{24,20},{28,24},{0,28},{5,1},{9... | collective-permute-start | bytes 49160 | tf_op jit(solution)/shard_map/ppermute | solution.py:18
  91.8 2.8 %fusion.58 = bf16[3,3,8,32,8,32]{5,3,4,2,1,0:T(8,128)(2,1)S(1)} fusion(bf16[3,3,8,32,512,1]{4,3,5,2,1,0:T(8,128)(2,1)S(1)} %bitcast.302, bf16[8,32,512,1,1,1]{2,1,0,5,4,3:T(8,128)(2,1)S(1)} %bitcast.339), kind=kOutput, calls=%fused_computation.227 | convolution fusion | flops 603979776 | bytes 3801088 | tf_op jit(solution)/shard_map/dot_general | solution.py:88
  96.4 2.6 %collective-permute-start.17 = (bf16[1,32,256]{2,1,0:T(8,128)(2,1)}, bf16[1,32,256]{2,1,0:T(8,128)(2,1)}, u32[]{:S(2)}, u32[]{:S(2)}) collective-permute-start(bf16[1,32,256]{2,1,0:T(8,128)(2,1)} %get-tuple-element.74), channel_id=1, source_target_pairs={{4,0},{8,4},{12,8},{16,12},{20,16},{24,20},{28,24},{0,28},{5,1},{9... | collective-permute-start | bytes 49160 | tf_op jit(solution)/shard_map/ppermute | solution.py:18
  99.9 3.8 %collective-permute-start.11 = (bf16[18,1,256]{2,1,0:T(2,128)(2,1)S(1)}, bf16[18,1,256]{2,1,0:T(2,128)(2,1)S(1)}, u32[]{:S(2)}, u32[]{:S(2)}) collective-permute-start(bf16[18,1,256]{2,1,0:T(2,128)(2,1)S(1)} %get-tuple-element.71), channel_id=1, source_target_pairs={{1,0},{2,1},{3,2},{0,3},{5,4},{6,5},{7,6},{4,7},{9,8},{10,9},{11,1... | collective-permute-start | bytes 27656 | tf_op jit(solution)/shard_map/ppermute | solution.py:18
  103.7 1.7 collective-permute-done.10
  107.6 2.4 %copy.58 = bf16[512,2304]{0,1:T(8,128)(2,1)} copy(bf16[512,2304]{1,0:T(8,128)(2,1)S(1)} %bitcast.300) | data formatting | bytes 4718592 | tf_op jit(solution)/shard_map/reshape | solution.py:77
  110.1 4.5 %fusion.62 = bf16[3,3,8,32,8,32]{5,3,4,2,1,0:T(8,128)(2,1)S(1)} fusion(bf16[3,3,8,32,512,1]{4,3,5,2,1,0:T(8,128)(2,1)} %bitcast.303, bf16[8,32,512,1,1,1]{2,1,0,5,4,3:T(8,128)(2,1)S(1)} %bitcast.338), kind=kOutput, calls=%fused_computation.231 | convolution fusion | flops 603979776 | bytes 3801088 | tf_op jit(solution)/shard_map/dot_general | solution.py:88
  116.9 2.1 pad.4
  119.0 5.2 %all-to-all-start = ((f32[32,56,128]{2,1,0:T(8,128)}), f32[32,56,128]{2,1,0:T(8,128)S(1)}, u32[]{:S(2)}, u32[]{:S(2)}) async-start(f32[32,56,128]{2,1,0:T(8,128)} %bitcast.144), calls=%async_computation | async-start | bytes 1835008 | tf_op jit(solution)/shard_map/all_to_all | solution.py:122
  125.0 1.8 collective-permute-start.18
  126.8 2.2 collective-permute-start.19
  129.0 2.8 %fusion.19 = bf16[16,32,256]{2,1,0:T(8,128)(2,1)} fusion(bf16[16,32,2304]{2,1,0:T(8,128)(2,1)S(1)} %slice_dynamic-update-slice_fusion.12, bf16[2304,256,1]{1,0,2:T(8,128)(2,1)} %bitcast.320, bf16[16,32,256]{2,1,0:T(8,128)(2,1)} %param.7), kind=kOutput, calls=%fused_computation.24 | convolution fusion | flops 604372992 | bytes 4063232 | tf_op jit(solution)/shard_map/dot_general | solution.py:83
  131.7 12.5 %collective-permute-done.18 = bf16[18,1,256]{2,1,0:T(2,128)(2,1)S(1)} collective-permute-done((bf16[18,1,256]{2,1,0:T(2,128)(2,1)S(1)}, bf16[18,1,256]{2,1,0:T(2,128)(2,1)S(1)}, u32[]{:S(2)}, u32[]{:S(2)}) %collective-permute-start.18) | collective-permute-done | bytes 9248 | tf_op jit(solution)/shard_map/ppermute | solution.py:15
  147.2 1.5 fusion.21
  148.8 76.1 %all_gather.3 = f32[1792,128]{1,0:T(8,128)S(1)} all-gather(f32[56,128]{1,0:T(8,128)S(1)} %broadcast_multiply_fusion), channel_id=1, replica_groups=mesh['gx'=8,'gy'=4] {'gx','gy'}, dimensions={0}, use_global_device_ids=true | all-gather | bytes 946176 | tf_op jit(solution)/shard_map/all_gather | solution.py:123
  (279 shorter events, 62.9 us)
Async XLA Ops:
  0.6 14.0 %copy-start = (bf16[2,2,2,32,64]{4,3,2,1,0:T(8,128)(2,1)S(1)}, bf16[2,2,2,32,64]{4,3,2,1,0:T(8,128)(2,1)}, u32[]{:S(2)}) copy-start(bf16[2,2,2,32,64]{4,3,2,1,0:T(8,128)(2,1)} %param.9) | copy-start | bytes 98308
  0.6 11.4 %copy-start.18 = (bf16[3,3,3,32,32]{4,3,2,1,0:T(8,128)(2,1)S(1)}, bf16[3,3,3,32,32]{4,3,2,1,0:T(8,128)(2,1)}, u32[]{:S(2)}) copy-start(bf16[3,3,3,32,32]{4,3,2,1,0:T(8,128)(2,1)} %param.8) | copy-start | bytes 165892
  3.3 24.2 %collective-permute-start = (bf16[1,32,512]{2,1,0:T(8,128)(2,1)}, bf16[1,32,512]{2,1,0:T(8,128)(2,1)}, u32[]{:S(2)}, u32[]{:S(2)}) collective-permute-start(bf16[1,32,512]{2,1,0:T(8,128)(2,1)} %get-tuple-element.51), channel_id=1, source_target_pairs={{0,4},{4,8},{8,12},{12,16},{16,20},{20,24},{24,28},{28,0},{1,5},{5... | collective-permute-start | bytes 98312 | tf_op jit(solution)/shard_map/ppermute | solution.py:15
  3.8 23.8 %collective-permute-start.1 = (bf16[1,32,512]{2,1,0:T(8,128)(2,1)}, bf16[1,32,512]{2,1,0:T(8,128)(2,1)}, u32[]{:S(2)}, u32[]{:S(2)}) collective-permute-start(bf16[1,32,512]{2,1,0:T(8,128)(2,1)} %get-tuple-element.52), channel_id=1, source_target_pairs={{4,0},{8,4},{12,8},{16,12},{20,16},{24,20},{28,24},{0,28},{5,1},{9... | collective-permute-start | bytes 98312 | tf_op jit(solution)/shard_map/ppermute | solution.py:18
  11.8 4.7 %copy-start.7 = (bf16[3,3,3,64,64]{4,3,2,1,0:T(8,128)(2,1)S(1)}, bf16[3,3,3,64,64]{4,3,2,1,0:T(8,128)(2,1)}, u32[]{:S(2)}) copy-start(bf16[3,3,3,64,64]{4,3,2,1,0:T(8,128)(2,1)} %param.10) | copy-start | bytes 663556
  28.4 6.6 %collective-permute-start.2 = (bf16[18,1,512]{2,1,0:T(2,128)(2,1)S(1)}, bf16[18,1,512]{2,1,0:T(2,128)(2,1)S(1)}, u32[]{:S(2)}, u32[]{:S(2)}) collective-permute-start(bf16[18,1,512]{2,1,0:T(2,128)(2,1)S(1)} %get-tuple-element.46), channel_id=1, source_target_pairs={{0,1},{1,2},{2,3},{3,0},{4,5},{5,6},{6,7},{7,4},{8,9},{9,10},{10,1... | collective-permute-start | bytes 55304 | tf_op jit(solution)/shard_map/ppermute | solution.py:15
  30.7 4.4 %collective-permute-start.3 = (bf16[18,1,512]{2,1,0:T(2,128)(2,1)S(1)}, bf16[18,1,512]{2,1,0:T(2,128)(2,1)S(1)}, u32[]{:S(2)}, u32[]{:S(2)}) collective-permute-start(bf16[18,1,512]{2,1,0:T(2,128)(2,1)S(1)} %get-tuple-element.45), channel_id=1, source_target_pairs={{1,0},{2,1},{3,2},{0,3},{5,4},{6,5},{7,6},{4,7},{9,8},{10,9},{11,1... | collective-permute-start | bytes 55304 | tf_op jit(solution)/shard_map/ppermute | solution.py:18
  45.0 4.0 %collective-permute-start.4 = (bf16[1,16,256]{2,1,0:T(8,128)(2,1)S(1)}, bf16[1,16,256]{2,1,0:T(8,128)(2,1)S(1)}, u32[]{:S(2)}, u32[]{:S(2)}) collective-permute-start(bf16[1,16,256]{2,1,0:T(8,128)(2,1)S(1)} %get-tuple-element.89), channel_id=1, source_target_pairs={{0,4},{4,8},{8,12},{12,16},{16,20},{20,24},{24,28},{28,0},{1,5},{5... | collective-permute-start | bytes 24584 | tf_op jit(solution)/shard_map/ppermute | solution.py:15
  45.0 4.0 %collective-permute-start.5 = (bf16[1,16,256]{2,1,0:T(8,128)(2,1)S(1)}, bf16[1,16,256]{2,1,0:T(8,128)(2,1)S(1)}, u32[]{:S(2)}, u32[]{:S(2)}) collective-permute-start(bf16[1,16,256]{2,1,0:T(8,128)(2,1)S(1)} %get-tuple-element.90), channel_id=1, source_target_pairs={{4,0},{8,4},{12,8},{16,12},{20,16},{24,20},{28,24},{0,28},{5,1},{9... | collective-permute-start | bytes 24584 | tf_op jit(solution)/shard_map/ppermute | solution.py:18
  49.6 9.1 %collective-permute-start.6 = (bf16[10,1,256]{2,1,0:T(2,128)(2,1)}, bf16[10,1,256]{2,1,0:T(2,128)(2,1)S(1)}, u32[]{:S(2)}, u32[]{:S(2)}) collective-permute-start(bf16[10,1,256]{2,1,0:T(2,128)(2,1)} %get-tuple-element.84), channel_id=1, source_target_pairs={{0,1},{1,2},{2,3},{3,0},{4,5},{5,6},{6,7},{7,4},{8,9},{9,10},{10,1... | collective-permute-start | bytes 15368 | tf_op jit(solution)/shard_map/ppermute | solution.py:15
  50.8 8.0 %collective-permute-start.7 = (bf16[10,1,256]{2,1,0:T(2,128)(2,1)S(1)}, bf16[10,1,256]{2,1,0:T(2,128)(2,1)S(1)}, u32[]{:S(2)}, u32[]{:S(2)}) collective-permute-start(bf16[10,1,256]{2,1,0:T(2,128)(2,1)S(1)} %get-tuple-element.83), channel_id=1, source_target_pairs={{1,0},{2,1},{3,2},{0,3},{5,4},{6,5},{7,6},{4,7},{9,8},{10,9},{11,1... | collective-permute-start | bytes 15368 | tf_op jit(solution)/shard_map/ppermute | solution.py:18
  66.5 4.9 %copy-start.40 = (pred[4,4,1,1,1,1,1]{1,0,2,3,4,5,6:T(4,128)(4,1)S(1)}, pred[4,4,1,1,1,1,1]{1,0,2,3,4,5,6:T(4,128)(4,1)}, u32[]{:S(2)}) copy-start(pred[4,4,1,1,1,1,1]{1,0,2,3,4,5,6:T(4,128)(4,1)} %fusion.48) | copy-start | bytes 52
  68.2 7.8 %collective-permute-start.12 = (bf16[1,16,256]{2,1,0:T(8,128)(2,1)S(1)}, bf16[1,16,256]{2,1,0:T(8,128)(2,1)S(1)}, u32[]{:S(2)}, u32[]{:S(2)}) collective-permute-start(bf16[1,16,256]{2,1,0:T(8,128)(2,1)S(1)} %get-tuple-element.85), channel_id=1, source_target_pairs={{0,4},{4,8},{8,12},{12,16},{16,20},{20,24},{24,28},{28,0},{1,5},{5... | collective-permute-start | bytes 24584 | tf_op jit(solution)/shard_map/ppermute | solution.py:15
  68.3 7.7 %collective-permute-start.13 = (bf16[1,16,256]{2,1,0:T(8,128)(2,1)S(1)}, bf16[1,16,256]{2,1,0:T(8,128)(2,1)S(1)}, u32[]{:S(2)}, u32[]{:S(2)}) collective-permute-start(bf16[1,16,256]{2,1,0:T(8,128)(2,1)S(1)} %get-tuple-element.86), channel_id=1, source_target_pairs={{4,0},{8,4},{12,8},{16,12},{20,16},{24,20},{28,24},{0,28},{5,1},{9... | collective-permute-start | bytes 24584 | tf_op jit(solution)/shard_map/ppermute | solution.py:18
  76.0 8.5 %collective-permute-start.14 = (bf16[10,1,256]{2,1,0:T(2,128)(2,1)S(1)}, bf16[10,1,256]{2,1,0:T(2,128)(2,1)S(1)}, u32[]{:S(2)}, u32[]{:S(2)}) collective-permute-start(bf16[10,1,256]{2,1,0:T(2,128)(2,1)S(1)} %get-tuple-element.80), channel_id=1, source_target_pairs={{0,1},{1,2},{2,3},{3,0},{4,5},{5,6},{6,7},{7,4},{8,9},{9,10},{10,1... | collective-permute-start | bytes 15368 | tf_op jit(solution)/shard_map/ppermute | solution.py:15
  76.1 8.4 %collective-permute-start.15 = (bf16[10,1,256]{2,1,0:T(2,128)(2,1)S(1)}, bf16[10,1,256]{2,1,0:T(2,128)(2,1)S(1)}, u32[]{:S(2)}, u32[]{:S(2)}) collective-permute-start(bf16[10,1,256]{2,1,0:T(2,128)(2,1)S(1)} %get-tuple-element.79), channel_id=1, source_target_pairs={{1,0},{2,1},{3,2},{0,3},{5,4},{6,5},{7,6},{4,7},{9,8},{10,9},{11,1... | collective-permute-start | bytes 15368 | tf_op jit(solution)/shard_map/ppermute | solution.py:18
  80.7 4.0 %copy-start.43 = (f32[8,16,256]{2,1,0:T(8,128)S(1)}, f32[8,16,256]{2,1,0:T(8,128)}, u32[]{:S(2)}) copy-start(f32[8,16,256]{2,1,0:T(8,128)} %get-tuple-element.108) | copy-start | bytes 393220
  81.8 17.3 %collective-permute-start.8 = (bf16[1,32,256]{2,1,0:T(8,128)(2,1)}, bf16[1,32,256]{2,1,0:T(8,128)(2,1)}, u32[]{:S(2)}, u32[]{:S(2)}) collective-permute-start(bf16[1,32,256]{2,1,0:T(8,128)(2,1)} %get-tuple-element.75), channel_id=1, source_target_pairs={{0,4},{4,8},{8,12},{12,16},{16,20},{20,24},{24,28},{28,0},{1,5},{5... | collective-permute-start | bytes 49160 | tf_op jit(solution)/shard_map/ppermute | solution.py:15
  81.8 17.3 %collective-permute-start.9 = (bf16[1,32,256]{2,1,0:T(8,128)(2,1)}, bf16[1,32,256]{2,1,0:T(8,128)(2,1)S(1)}, u32[]{:S(2)}, u32[]{:S(2)}) collective-permute-start(bf16[1,32,256]{2,1,0:T(8,128)(2,1)} %get-tuple-element.76), channel_id=1, source_target_pairs={{4,0},{8,4},{12,8},{16,12},{20,16},{24,20},{28,24},{0,28},{5,1},{9... | collective-permute-start | bytes 49160 | tf_op jit(solution)/shard_map/ppermute | solution.py:18
  87.1 4.7 %copy-start.2 = (bf16[512,2304]{0,1:T(8,128)(2,1)S(1)}, bf16[512,2304]{0,1:T(8,128)(2,1)}, u32[]{:S(2)}) copy-start(bf16[512,2304]{0,1:T(8,128)(2,1)} %copy.46) | copy-start | bytes 7077892
  94.7 4.4 %copy-start.8 = (f32[864,128]{1,0:T(8,128)S(1)}, f32[864,128]{1,0:T(8,128)}, u32[]{:S(2)}) copy-start(f32[864,128]{1,0:T(8,128)} %reshape.690) | copy-start | bytes 1327108
  96.4 27.8 %collective-permute-start.16 = (bf16[1,32,256]{2,1,0:T(8,128)(2,1)}, bf16[1,32,256]{2,1,0:T(8,128)(2,1)}, u32[]{:S(2)}, u32[]{:S(2)}) collective-permute-start(bf16[1,32,256]{2,1,0:T(8,128)(2,1)} %get-tuple-element.73), channel_id=1, source_target_pairs={{0,4},{4,8},{8,12},{12,16},{16,20},{20,24},{24,28},{28,0},{1,5},{5... | collective-permute-start | bytes 49160 | tf_op jit(solution)/shard_map/ppermute | solution.py:15
  96.4 27.8 %collective-permute-start.17 = (bf16[1,32,256]{2,1,0:T(8,128)(2,1)}, bf16[1,32,256]{2,1,0:T(8,128)(2,1)}, u32[]{:S(2)}, u32[]{:S(2)}) collective-permute-start(bf16[1,32,256]{2,1,0:T(8,128)(2,1)} %get-tuple-element.74), channel_id=1, source_target_pairs={{4,0},{8,4},{12,8},{16,12},{20,16},{24,20},{28,24},{0,28},{5,1},{9... | collective-permute-start | bytes 49160 | tf_op jit(solution)/shard_map/ppermute | solution.py:18
  99.8 5.6 %collective-permute-start.10 = (bf16[18,1,256]{2,1,0:T(2,128)(2,1)S(1)}, bf16[18,1,256]{2,1,0:T(2,128)(2,1)S(1)}, u32[]{:S(2)}, u32[]{:S(2)}) collective-permute-start(bf16[18,1,256]{2,1,0:T(2,128)(2,1)S(1)} %get-tuple-element.72), channel_id=1, source_target_pairs={{0,1},{1,2},{2,3},{3,0},{4,5},{5,6},{6,7},{7,4},{8,9},{9,10},{10,1... | collective-permute-start | bytes 27656 | tf_op jit(solution)/shard_map/ppermute | solution.py:15
  99.9 5.6 %collective-permute-start.11 = (bf16[18,1,256]{2,1,0:T(2,128)(2,1)S(1)}, bf16[18,1,256]{2,1,0:T(2,128)(2,1)S(1)}, u32[]{:S(2)}, u32[]{:S(2)}) collective-permute-start(bf16[18,1,256]{2,1,0:T(2,128)(2,1)S(1)} %get-tuple-element.71), channel_id=1, source_target_pairs={{1,0},{2,1},{3,2},{0,3},{5,4},{6,5},{7,6},{4,7},{9,8},{10,9},{11,1... | collective-permute-start | bytes 27656 | tf_op jit(solution)/shard_map/ppermute | solution.py:18
  110.1 4.5 %copy-start.27 = (pred[1,8,8]{2,0,1:T(4,128)(4,1)S(1)}, pred[1,8,8]{2,0,1:T(4,128)(4,1)}, u32[]{:S(2)}) copy-start(pred[1,8,8]{2,0,1:T(4,128)(4,1)} %iota_compare_fusion.4) | copy-start | bytes 196
  110.1 4.5 %copy-start.29 = (pred[1,8,8]{2,0,1:T(4,128)(4,1)S(1)}, pred[1,8,8]{2,0,1:T(4,128)(4,1)}, u32[]{:S(2)}) copy-start(pred[1,8,8]{2,0,1:T(4,128)(4,1)} %get-tuple-element.128) | copy-start | bytes 196
  110.1 4.5 %copy-start.31 = (pred[1,8,8]{2,0,1:T(4,128)(4,1)S(1)}, pred[1,8,8]{2,0,1:T(4,128)(4,1)}, u32[]{:S(2)}) copy-start(pred[1,8,8]{2,0,1:T(4,128)(4,1)} %get-tuple-element.129) | copy-start | bytes 196
  119.0 29.7 %all-to-all-start = ((f32[32,56,128]{2,1,0:T(8,128)}), f32[32,56,128]{2,1,0:T(8,128)S(1)}, u32[]{:S(2)}, u32[]{:S(2)}) async-start(f32[32,56,128]{2,1,0:T(8,128)} %bitcast.144), calls=%async_computation | async-start | bytes 1835008 | tf_op jit(solution)/shard_map/all_to_all | solution.py:122
  125.0 19.3 %collective-permute-start.18 = (bf16[18,1,256]{2,1,0:T(2,128)(2,1)S(1)}, bf16[18,1,256]{2,1,0:T(2,128)(2,1)S(1)}, u32[]{:S(2)}, u32[]{:S(2)}) collective-permute-start(bf16[18,1,256]{2,1,0:T(2,128)(2,1)S(1)} %get-tuple-element.68), channel_id=1, source_target_pairs={{0,1},{1,2},{2,3},{3,0},{4,5},{5,6},{6,7},{7,4},{8,9},{9,10},{10,1... | collective-permute-start | bytes 27656 | tf_op jit(solution)/shard_map/ppermute | solution.py:15
  126.8 17.5 %collective-permute-start.19 = (bf16[18,1,256]{2,1,0:T(2,128)(2,1)S(1)}, bf16[18,1,256]{2,1,0:T(2,128)(2,1)S(1)}, u32[]{:S(2)}, u32[]{:S(2)}) collective-permute-start(bf16[18,1,256]{2,1,0:T(2,128)(2,1)S(1)} %get-tuple-element.67), channel_id=1, source_target_pairs={{1,0},{2,1},{3,2},{0,3},{5,4},{6,5},{7,6},{4,7},{9,8},{10,9},{11,1... | collective-permute-start | bytes 27656 | tf_op jit(solution)/shard_map/ppermute | solution.py:18
  148.8 80.8 %copy-start.1 = (bf16[2,2,2,32,64]{4,3,2,1,0:T(8,128)(2,1)S(1)}, bf16[2,2,2,32,64]{4,3,2,1,0:T(8,128)(2,1)}, u32[]{:S(2)}) copy-start(bf16[2,2,2,32,64]{4,3,2,1,0:T(8,128)(2,1)} %param.9) | copy-start | bytes 98308
  (34 other events, 65.4 us)
where the time goes:
time: 231 us; the launch traced here: 230 us
  blocking collectives  76.1 us (33%)
  starting transfers between devices  39.2 us (17%)
  matrix products  36.7 us (16%)
  local copies, waits for them, and re-layouts  33.6 us (15%)
  other arithmetic  24.1 us (10%)
  waiting for transfers between devices  17.8 us (8%)
    all_gather x1, blocking collectives, summed_over(): lax.all_gather(jnp.sum(pieces, axis=0) * scale, axes, axis=0, tiled=True)  76.1 us
    ppermute x10, starting transfers between devices, padded_2(): lax.ppermute(lax.slice_in_dim(block, 0, width, axis=dim), axis, backward)  28 us
    ppermute x10, waiting for transfers between devices, padded_2(): lax.ppermute(lax.slice_in_dim(block, block.shape[dim] - width, None, axis...  17.6 us
    dot_general x6, matrix products, conv_padded(): jnp.dot(columns(padded), band, preferred_element_type=jnp.float32)  11.2 us
    dot_general x3, matrix products, weight_grad(): lax.dot_general(columns(padded), flat, (((0,), (0,)), ((), ())), preferre...  8.12 us
    unnamed x126, local copies, waits for them, and re-layouts  6.85 us
    concatenate x10, other arithmetic, padded_2(): block = jnp.concatenate([low, block, high], axis=dim)  6.2 us
    ppermute x10, starting transfers between devices, padded_2(): lax.ppermute(lax.slice_in_dim(block, block.shape[dim] - width, None, axis...  6.11 us
  transfers between devices with their start and end apart: 21, of which 5 were waited for; matrix products, arithmetic and copies ran while one was open for 29% of the time, Pallas kernels for 0%

commit v1 on v0

v1 whole, which is shorter than its diff:
```python
import functools
import math

import jax
import jax.numpy as jnp
from jax import lax
from jax.experimental import pallas as pl
from jax.experimental.pallas import tpu as pltpu
from jax.sharding import PartitionSpec as P

BF16 = jnp.bfloat16
F32 = jnp.float32
MESH = pl.DeviceIdType.MESH
LANES = 128
ROWS = 16


def dot(left, right):
    return lax.dot_general(left, right, (((1,), (0,)), ((), ())), preferred_element_type=F32)


def dot_t(left, right):
    return lax.dot_general(left, right, (((1,), (1,)), ((), ())), preferred_element_type=F32)


def iota(shape, dim):
    return lax.broadcasted_iota(jnp.int32, shape, dim)


def div(value, by):
    return lax.div(value, jnp.int32(by))


def rem(value, by):
    return lax.rem(value, jnp.int32(by))


def one_hot(mask):
    return jnp.where(mask, 1.0, 0.0).astype(BF16)


def silu_parts(value):
    sig = jax.nn.sigmoid(value)
    return value * sig, sig * (1.0 + value * (1.0 - sig))


def split_matrix(xh, ys, parity):
    hy = ys // 2
    shape = (xh * hy, xh * ys)
    row, col = iota(shape, 0), iota(shape, 1)
    return one_hot(col == div(row, hy) * ys + rem(row, hy) * 2 + parity)


def merge_matrix(xh, ys, parity):
    hy = ys // 2
    shape = (xh * ys, xh * hy)
    row, col = iota(shape, 0), iota(shape, 1)
    same = col == div(row, ys) * hy + div(rem(row, ys), 2)
    return one_hot(same & (rem(row, 2) == parity))


def shift_matrix(rows, hy, step):
    row, col = iota((rows, rows), 0), iota((rows, rows), 1)
    edge = hy - 1 if step > 0 else 0
    return one_hot((col == row + step) & (rem(row, hy) != edge))


def place_matrix(count, part, hy, step):
    rows = (count + 2) // 2 * hy
    shape = (rows, 3 * ROWS)
    row, col = iota(shape, 0), iota(shape, 1)
    across = div(row, hy) + part * ((count + 2) // 2)
    edge = hy - 1 if step > 0 else 0
    wanted = jnp.where(
        across == 0, count - 1, jnp.where(across == count + 1, 2 * ROWS, across + ROWS - 1)
    )
    return one_hot((rem(row, hy) == edge) & (col == wanted))


def edge_matrix(count, hy, last):
    shape = (ROWS, count * hy)
    row, col = iota(shape, 0), iota(shape, 1)
    return one_hot(col == row * hy + (hy - 1 if last else 0))


def tile_matrix(small, width):
    shape = (small, width)
    return one_hot(rem(iota(shape, 1), small) == iota(shape, 0))


def build_band(weight, band, planes, chan, width):
    tile = tile_matrix(chan, width)
    plane = div(iota((chan, width), 1), chan)

    def step(tap, carry):
        start = pl.multiple_of(tap * (3 * chan), ROWS)
        wide = dot(weight[pl.ds(start, 3 * chan), :], tile)
        parts = [wide[kk * chan : (kk + 1) * chan] for kk in range(3)]
        for pp in range(planes):
            block = jnp.zeros((chan, width), F32)
            for kk in range(3):
                block = jnp.where(plane == pp + 1 - kk, parts[kk], block)
            band[tap, pp * chan : (pp + 1) * chan, :] = block.astype(BF16)
        return carry

    lax.fori_loop(0, 9, step, 0)


def build_pool(weight, mats, half, cf, cc, width):
    wide = dot(weight[...], tile_matrix(cc, width))
    plane = div(iota((2 * cf, width), 1), cc)
    for ij in range(4):
        part = wide[ij * 2 * cf : (ij + 1) * 2 * cf]
        for zz in range(half):
            block = jnp.where(plane == zz, part, 0.0)
            mats[ij, zz * 2 * cf : (zz + 1) * 2 * cf, :] = block.astype(BF16)


def build_unpool(weight, mats, half, cf, cc, width):
    wide = dot(weight[...], tile_matrix(cf, width))
    lane = iota((cc, width), 1)
    plane = div(lane, 2 * cf)
    upper = rem(div(lane, cf), 2) == 1
    for ij in range(4):
        low = wide[2 * ij * cc : (2 * ij + 1) * cc]
        high = wide[(2 * ij + 1) * cc : (2 * ij + 2) * cc]
        part = jnp.where(upper, high, low)
        for zz in range(half):
            block = jnp.where(plane == zz, part, 0.0)
            mats[ij, zz * cc : (zz + 1) * cc, :] = block.astype(BF16)


def parity_rows(value, hx, hy, side):
    width = value.shape[-1]
    return value.reshape(hx, 2, hy, width)[:, side].reshape(hx * hy, width)


def woven_rows(first, second, hx, hy):
    width = first.shape[-1]
    both = jnp.concatenate(
        [first.reshape(hx, 1, hy, width), second.reshape(hx, 1, hy, width)], axis=1
    )
    return both.reshape(2 * hx * hy, width)


def folded(block, chan):
    total = block[:, :LANES]
    for part in range(1, block.shape[1] // LANES):
        total = total + block[:, part * LANES : (part + 1) * LANES]
    step = LANES // 2
    while step >= chan:
        total = total + pltpu.roll(total, step, 1)
        step //= 2
    return total


class Packer:
    def __init__(self, target, row, chan):
        self.target, self.row, self.chan = target, row, chan
        self.per = LANES // chan
        self.group = div(iota((chan, LANES), 1), chan)
        self.held, self.count = None, 0

    def add(self, value):
        spot = self.count % self.per
        self.held = value if spot == 0 else jnp.where(self.group == spot, value, self.held)
        self.count += 1
        if spot == self.per - 1:
            self.flush()

    def flush(self):
        if self.held is not None:
            self.target[self.row : self.row + self.chan, :] = self.held.astype(BF16)
            self.row += self.chan
            self.held = None
        return self.row


def conv_grad(parts, tap_of, planes, chan, width, packer):
    plane = div(iota((chan, width), 1), chan)
    for tap in range(9):
        dband = None
        for index, part in enumerate(parts):
            term = dot(part, tap_of(index, tap // 3, tap % 3))
            dband = term if dband is None else dband + term
        for kk in range(3):
            total = jnp.zeros((chan, width), F32)
            for zz in range(planes):
                if 0 <= zz + kk - 1 < planes:
                    rows = dband[zz * chan : (zz + 1) * chan]
                    total = jnp.where(plane == zz + kk - 1, rows, total)
            packer.add(folded(total, chan))
    return packer.flush()


def pair_grad(left_t, rights, half, chan, width, packer):
    plane = div(iota((chan, width), 1), width // half)
    for right in rights:
        full = dot(left_t, right)
        total = jnp.zeros((chan, width), F32)
        for zz in range(half):
            total = jnp.where(plane == zz, full[zz * chan : (zz + 1) * chan], total)
        packer.add(folded(total, width // half))
    return packer.flush()


def turned(value):
    return value.astype(F32).T.astype(BF16)


def main_kernel(
    dims, fields, w_down, w_pool, w_mid, w_unpool, w_up, cot,
    out_s, gf_s, grads,
    fc, sk, dd, co, dm,
    fc_send, sk_send, dd_send, co_send, dm_send,
    fc_recv, sk_recv, dd_recv, co_recv, dm_recv,
    b_down, b_up, b_mid, p_mat, u_mat,
    shift, place, place_c,
    hid, ds_down, g_up, d_up, cot_t,
    sum0, sum1, sum2, got0, got1, got2, mid0, mid1, mid2,
    ex_send, ex_recv, s1, r1, s2, r2, s3, r3,
):
    nx, ny, xs, ys, cf, cc, planes, scale, sizes = dims
    half, hx, hy = planes // 2, xs // 2, ys // 2
    width = planes * cf
    cells, ccells = xs * hy, hx * hy
    ix, iy = lax.axis_index("gx"), lax.axis_index("gy")

    def at(dx, dy):
        return {"gx": lax.rem(ix + (dx + nx), nx), "gy": lax.rem(iy + (dy + ny), ny)}

    partners = [(dx, 0) for dx in range(1, nx)] + [(0, dy) for dy in range(1, ny)]
    partners += [(dx, dy) for dx in (-1, 1) for dy in (-1, 1)]
    barrier = pltpu.get_barrier_semaphore()
    for dx, dy in partners:
        pl.semaphore_signal(barrier, inc=1, device_id=at(dx, dy), device_id_type=MESH)

    def send(src, dst, ssem, rsem, dx, dy):
        copy = pltpu.make_async_remote_copy(
            src_ref=src, dst_ref=dst, send_sem=ssem, recv_sem=rsem,
            device_id=at(dx, dy), device_id_type=MESH,
        )
        copy.start()
        return copy

    def exchange(number, buf, snd, rcv, count, low, high):
        ss, rs = ex_send.at[number], ex_recv.at[number]
        copies = []
        for dx in (-1, 0, 1):
            rows = pl.ds((1 - dx) * ROWS, ROWS)
            for side, dy in ((0, -1), (1, 1)):
                spot = 2 * (dx + 1) + side
                copies.append(
                    send(snd.at[side], rcv.at[side, :, rows, :], ss.at[spot], rs.at[spot], dx, dy)
                )
        for spot, dx, src, dst in ((6, -1, 1, count + 1), (7, 1, count, 0)):
            copies.append(
                send(
                    buf.at[:, src, :, low:high], buf.at[:, dst, :, low:high],
                    ss.at[spot], rs.at[spot], dx, 0,
                )
            )
        return copies

    def arrive(copies):
        for copy in copies:
            copy.wait_recv()

    def shifts(buf, rcv, index, count, up_from, up_to, down_from, down_to, places):
        part = (count + 2) // 2
        rows = part * hy
        for hh in range(2):
            span = slice(hh * part, (hh + 1) * part)
            for side, start, stop in ((0, up_from, up_to), (1, down_from, down_to)):
                own = buf[index, span, :, start : start + width].reshape(rows, width)
                moved = dot(shift[side, :rows, :rows], own)
                moved = moved + dot(places[side, hh], rcv[side, index])
                buf[index, span, :, stop : stop + width] = moved.astype(BF16).reshape(
                    part, hy, width
                )

    def fine_shifts(buf, rcv, index=0):
        shifts(buf, rcv, index, xs, width, 3 * width, 2 * width, 0, place)

    def coarse_shifts(buf, rcv):
        shifts(buf, rcv, 0, hx, width, 2 * width, width, 0, place_c)

    def tap(buf, index, count, aa, lane):
        return buf[index, aa : aa + count, :, lane : lane + width].reshape(count * hy, width)

    def conv(buf, index, count, jj, band):
        total = None
        for aa in range(3):
            left = buf[index, aa : aa + count, :, jj * width : (jj + 3) * width]
            term = dot(
                left.reshape(count * hy, 3 * width),
                band[3 * aa : 3 * aa + 3].reshape(3 * width, width),
            )
            total = term if total is None else total + term
        return total

    def conv_t(buf, index, count, jj, band):
        total = None
        for aa in range(3):
            for bb in range(3):
                left = tap(buf, index, count, aa, (jj + bb) * width)
                term = dot_t(left, band[3 * (2 - aa) + 2 - bb])
                total = term if total is None else total + term
        return total

    def edges(buf, snd, index, count, low, high):
        for side, lane in ((0, low), (1, high)):
            own = tap(buf, index, count, 1, lane)
            snd[side, index] = dot(edge_matrix(count, hy, side == 1), own).astype(BF16)

    for parity in range(2):
        pick = split_matrix(hx, ys, parity)
        for index, ref in ((0, fields), (1, cot)):
            for hh in range(2):
                rows = ref[hh * hx * ys : (hh + 1) * hx * ys, :]
                lane = (1 + parity) * width
                fc[index, 1 + hh * hx : 1 + (hh + 1) * hx, :, lane : lane + width] = (
                    dot(pick, rows).astype(BF16).reshape(hx, hy, width)
                )
    for index in range(2):
        edges(fc, fc_send, index, xs, width, 2 * width)
    pl.semaphore_wait(barrier, len(partners))
    moving = exchange(0, fc, fc_send, fc_recv, xs, width, 3 * width)

    part = (xs + 2) // 2 * hy
    for side, step in ((0, 1), (1, -1)):
        shift[side] = shift_matrix(part, hy, step)
        for hh in range(2):
            place[side, hh] = place_matrix(xs, hh, hy, step)
            place_c[side, hh] = place_matrix(hx, hh, hy, step)
    build_band(w_down, b_down, planes, cf, width)
    build_pool(w_pool, p_mat, half, cf, cc, width)
    build_band(w_up, b_up, planes, cf, width)
    for jj in range(2):
        cot_t[jj] = turned(tap(fc, 1, xs, 1, (1 + jj) * width))

    arrive(moving)
    sends = list(moving)
    fine_shifts(fc, fc_recv, 0)
    for jj in range(2):
        value, slope = silu_parts(conv(fc, 0, xs, jj, b_down))
        hid[jj] = value.astype(BF16)
        ds_down[jj] = slope
    pre_pool = None
    for jj in range(2):
        for ii in range(2):
            term = dot(parity_rows(hid[jj], hx, hy, ii), p_mat[2 * ii + jj])
            pre_pool = term if pre_pool is None else pre_pool + term
    coarse, ds_pool = silu_parts(pre_pool)
    co[0, 1 : hx + 1, :, width : 2 * width] = coarse.astype(BF16).reshape(hx, hy, width)
    edges(co, co_send, 0, hx, width, width)
    moving = exchange(1, co, co_send, co_recv, hx, width, 2 * width)

    build_band(w_mid, b_mid, half, cc, width)
    build_unpool(w_unpool, u_mat, half, cf, cc, width)
    fine_shifts(fc, fc_recv, 1)
    for jj in range(2):
        g_up[jj] = conv_t(fc, 1, xs, jj, b_up)

    arrive(moving)
    sends += moving
    coarse_shifts(co, co_recv)
    value, ds_mid = silu_parts(conv(co, 0, hx, 0, b_mid))
    own = tap(co, 0, hx, 1, width).astype(F32)
    middle = (own + value).astype(BF16)
    d_middle = None
    for jj in range(2):
        lifted = [dot(middle, u_mat[2 * ii + jj]) for ii in range(2)]
        pre_up = hid[jj].astype(F32) + woven_rows(lifted[0], lifted[1], hx, hy)
        value, slope = silu_parts(pre_up)
        lane = (1 + jj) * width
        sk[0, 1 : xs + 1, :, lane : lane + width] = value.astype(BF16).reshape(xs, hy, width)
        d_up[jj] = (g_up[jj] * slope).astype(BF16)
        for ii in range(2):
            term = dot_t(parity_rows(d_up[jj], hx, hy, ii), u_mat[2 * ii + jj])
            d_middle = term if d_middle is None else d_middle + term
    d_mid = (d_middle * ds_mid).astype(BF16)
    dm[0, 1 : hx + 1, :, width : 2 * width] = d_mid.reshape(hx, hy, width)
    edges(dm, dm_send, 0, hx, width, width)
    moving = exchange(2, dm, dm_send, dm_recv, hx, width, 2 * width)
    edges(sk, sk_send, 0, xs, width, 2 * width)
    skips = exchange(3, sk, sk_send, sk_recv, xs, width, 3 * width)

    class Reduction:
        def __init__(self, group, terms, got, mids, base):
            self.group, self.terms, self.got, self.mids, self.base = group, terms, got, mids, base
            self.rows = sizes[group] // nx

        def piece(self, index):
            return pl.ds(pl.multiple_of(index * self.rows, ROWS), self.rows)

        def scatter(self):
            self.copies = []
            for dx in range(1, nx):
                target = at(dx, 0)["gx"]
                self.copies.append(
                    send(
                        self.terms.at[self.piece(target), :], self.got.at[dx - 1],
                        s1.at[self.group, dx - 1], r1.at[self.group, dx - 1], dx, 0,
                    )
                )
            return self.copies

        def across(self):
            arrive(self.copies)
            total = self.terms[self.piece(ix), :].astype(F32)
            for dx in range(1, nx):
                total = total + self.got[dx - 1].astype(F32)
            self.mids[iy] = total.astype(BF16)
            self.copies = []
            for dy in range(1, ny):
                self.copies.append(
                    send(
                        self.mids.at[iy], self.mids.at[iy],
                        s2.at[self.group, dy - 1], r2.at[self.group, dy - 1], 0, dy,
                    )
                )
            return self.copies

        def gather(self):
            arrive(self.copies)
            total = self.mids[0].astype(F32)
            for yy in range(1, ny):
                total = total + self.mids[yy].astype(F32)
            start = pl.multiple_of(self.base + ix * self.rows, ROWS)
            mine = pl.ds(start, self.rows)
            grads[mine, :] = (total * scale).astype(BF16)
            self.copies = []
            for dx in range(1, nx):
                self.copies.append(
                    send(
                        grads.at[mine, :], grads.at[mine, :],
                        s3.at[self.group, dx - 1], r3.at[self.group, dx - 1], dx, 0,
                    )
                )
            return self.copies

    def padded_tail(ref, row, group):
        if row < sizes[group]:
            ref[row:, :] = jnp.zeros((sizes[group] - row, LANES), BF16)

    row = conv_grad(
        [turned(d_mid)], lambda index, aa, bb: tap(co, 0, hx, aa, bb * width),
        half, cc, width, Packer(sum0, 0, cc),
    )
    padded_tail(sum0, row, 0)
    red0 = Reduction(0, sum0, got0, mid0, 0)
    sends += red0.scatter()

    arrive(moving)
    sends += moving
    coarse_shifts(dm, dm_recv)
    d_coarse = d_middle + conv_t(dm, 0, hx, 0, b_mid)
    d_pool = (d_coarse * ds_pool).astype(BF16)
    for jj in range(2):
        back = [dot_t(d_pool, p_mat[2 * ii + jj]) for ii in range(2)]
        d_hidden = d_up[jj].astype(F32) + woven_rows(back[0], back[1], hx, hy)
        lane = (1 + jj) * width
        d_down = (d_hidden * ds_down[jj]).astype(BF16)
        dd[0, 1 : xs + 1, :, lane : lane + width] = d_down.reshape(xs, hy, width)
    edges(dd, dd_send, 0, xs, width, 2 * width)
    moving = exchange(4, dd, dd_send, dd_recv, xs, width, 3 * width)

    downs = [turned(tap(dd, 0, xs, 1, (1 + jj) * width)) for jj in range(2)]
    row = conv_grad(
        downs, lambda jj, aa, bb: tap(fc, 0, xs, aa, (jj + bb) * width),
        planes, cf, width, Packer(sum2, 0, cf),
    )
    row = pair_grad(
        turned(d_pool),
        [parity_rows(hid[jj], hx, hy, ii) for ii in range(2) for jj in range(2)],
        half, cc, width, Packer(sum2, row, cc),
    )
    padded_tail(sum2, row, 2)
    red2 = Reduction(2, sum2, got2, mid2, sizes[0] + sizes[1])
    sends += red2.scatter()
    sends += red0.across()

    arrive(skips)
    sends += skips
    fine_shifts(sk, sk_recv)
    row = conv_grad(
        [cot_t[0], cot_t[1]], lambda jj, aa, bb: tap(sk, 0, xs, aa, (jj + bb) * width),
        planes, cf, width, Packer(sum1, 0, cf),
    )
    row = pair_grad(
        turned(middle),
        [parity_rows(d_up[jj], hx, hy, ii) for ii in range(2) for jj in range(2)],
        half, cc, width, Packer(sum1, row, cc),
    )
    padded_tail(sum1, row, 1)
    red1 = Reduction(1, sum1, got1, mid1, sizes[0])
    sends += red1.scatter()
    sends += red2.across()
    sends += red0.gather()

    for jj in range(2):
        own = tap(fc, 0, xs, 1, (1 + jj) * width).astype(F32)
        out_s[jj] = (own + conv(sk, 0, xs, jj, b_up)).astype(BF16)
    sends += red1.across()
    sends += red2.gather()
    arrive(moving)
    sends += moving
    fine_shifts(dd, dd_recv)
    for jj in range(2):
        own = tap(fc, 1, xs, 1, (1 + jj) * width).astype(F32)
        gf_s[jj] = (own + conv_t(dd, 0, xs, jj, b_down)).astype(BF16)
    sends += red1.gather()
    for red in (red0, red1, red2):
        arrive(red.copies)
    for copy in sends:
        copy.wait_send()


def last_kernel(
    dims, out_s, gf_s, grads, output, grad_fields, g_down, g_pool, g_mid, g_unpool, g_up
):
    nx, ny, xs, ys, cf, cc, planes, scale, sizes = dims
    hx, hy = xs // 2, ys // 2
    merge = [merge_matrix(hx, ys, parity) for parity in range(2)]
    for source, target in ((out_s, output), (gf_s, grad_fields)):
        for hh in range(2):
            rows = slice(hh * hx * hy, (hh + 1) * hx * hy)
            value = dot(merge[0], source[0, rows, :]) + dot(merge[1], source[1, rows, :])
            target[hh * hx * ys : (hh + 1) * hx * ys, :] = value.astype(BF16)

    def unpack(row, chan, target):
        done, total = 0, target.shape[0]
        while done < total:
            block = grads[row : row + chan, :].astype(F32).T
            count = min(LANES, total - done)
            target[done : done + count, :] = block[:count]
            row, done = row + chan, done + count
        return row

    unpack(0, cc, g_mid)
    row = unpack(sizes[0], cf, g_up)
    for pair in range(2):
        block = grads[row : row + cc, :].astype(F32)
        for part in range(4):
            moved = block if part == 0 else pltpu.roll(block, LANES - part * cf, 1)
            first = (pair * 4 + part) * cc
            g_unpool[first : first + cc, :] = moved[:, :cf]
        row += cc
    row = unpack(sizes[0] + sizes[1], cf, g_down)
    unpack(row, cc, g_pool)


def per_device(dims, fields, w_down, w_pool, w_mid, w_unpool, w_up, cotangent):
    nx, ny, xs, ys, cf, cc, planes, scale, sizes = dims
    hx, hy = xs // 2, ys // 2
    width = planes * cf
    cells = xs * hy
    vmem = pl.BlockSpec(memory_space=pltpu.VMEM)

    def fine(lead=1):
        return pltpu.VMEM((lead, xs + 2, hy, 4 * width), BF16)

    def coarse():
        return pltpu.VMEM((1, hx + 2, hy, 3 * width), BF16)

    def sent(lead=1):
        return pltpu.VMEM((2, lead, ROWS, width), BF16)

    def taken(lead=1):
        return pltpu.VMEM((2, lead, 3 * ROWS, width), BF16)

    def sems(*shape):
        return pltpu.SemaphoreType.DMA(shape)

    part, part_c = (xs + 2) // 2 * hy, (hx + 2) // 2 * hy
    rows = [size // nx for size in sizes]
    split = jax.ShapeDtypeStruct((2, cells, width), BF16)
    out_s, gf_s, grads = pl.pallas_call(
        functools.partial(main_kernel, dims),
        out_shape=(split, split, jax.ShapeDtypeStruct((sum(sizes), LANES), BF16)),
        in_specs=[vmem] * 7,
        out_specs=(vmem,) * 3,
        scratch_shapes=[
            fine(2), fine(), fine(), coarse(), coarse(),
            sent(2), sent(), sent(), sent(), sent(),
            taken(2), taken(), taken(), taken(), taken(),
            pltpu.VMEM((9, width, width), BF16),
            pltpu.VMEM((9, width, width), BF16),
            pltpu.VMEM((9, width, width), BF16),
            pltpu.VMEM((4, width, width), BF16),
            pltpu.VMEM((4, width, width), BF16),
            pltpu.VMEM((2, part, part), BF16),
            pltpu.VMEM((2, 2, part, 3 * ROWS), BF16),
            pltpu.VMEM((2, 2, part_c, 3 * ROWS), BF16),
            pltpu.VMEM((2, cells, width), BF16),
            pltpu.VMEM((2, cells, width), F32),
            pltpu.VMEM((2, cells, width), F32),
            pltpu.VMEM((2, cells, width), BF16),
            pltpu.VMEM((2, width, cells), BF16),
            *[pltpu.VMEM((size, LANES), BF16) for size in sizes],
            *[pltpu.VMEM((nx - 1, row, LANES), BF16) for row in rows],
            *[pltpu.VMEM((ny, row, LANES), BF16) for row in rows],
            sems(5, 8), sems(5, 8),
            sems(3, nx - 1), sems(3, nx - 1),
            sems(3, ny - 1), sems(3, ny - 1),
            sems(3, nx - 1), sems(3, nx - 1),
        ],
        compiler_params=pltpu.CompilerParams(
            collective_id=0, has_side_effects=True, vmem_limit_bytes=56 << 20
        ),
        name="unet",
    )(
        fields.reshape(xs * ys, width),
        w_down.reshape(-1, cf),
        w_pool.reshape(-1, cc),
        w_mid.reshape(-1, cc),
        w_unpool.reshape(-1, cf),
        w_up.reshape(-1, cf),
        cotangent.reshape(xs * ys, width),
    )

    def f32(*shape):
        return jax.ShapeDtypeStruct(shape, F32)

    flat = jax.ShapeDtypeStruct((xs * ys, width), BF16)
    results = pl.pallas_call(
        functools.partial(last_kernel, dims),
        out_shape=(
            flat, flat, f32(27 * cf, cf), f32(8 * cf, cc), f32(27 * cc, cc),
            f32(8 * cc, cf), f32(27 * cf, cf),
        ),
        in_specs=[vmem] * 3,
        out_specs=(vmem,) * 7,
        name="layouts",
    )(out_s, gf_s, grads)
    shapes = [
        fields.shape, fields.shape, w_down.shape, w_pool.shape, w_mid.shape, w_unpool.shape,
        w_up.shape,
    ]
    return tuple(value.reshape(shape) for value, shape in zip(results, shapes))


def solution(mesh):
    nx, ny = mesh.shape["gx"], mesh.shape["gy"]

    def whole(fields, w_down, w_pool, w_mid, w_unpool, w_up, cotangent):
        cf, cc = w_down.shape[3], w_mid.shape[3]
        xs, ys = fields.shape[0] // nx, fields.shape[1] // ny
        planes = fields.shape[2] // cf
        scale = 1.0 / math.sqrt(fields.shape[0] * fields.shape[1] * planes)

        def blocks(taps, chan):
            return -(-taps * chan // LANES) * chan

        fine_rows = blocks(27, cf)
        pair_rows = 4 * cc * 2 * cf // LANES
        unit = ROWS * nx
        sizes = tuple(
            -(-rows // unit) * unit
            for rows in (blocks(27, cc), fine_rows + pair_rows, fine_rows + pair_rows)
        )
        dims = (nx, ny, xs, ys, cf, cc, planes, scale, sizes)
        placed = (P("gx", "gy", None), P(), P(), P(), P(), P(), P("gx", "gy", None))
        return jax.shard_map(
            functools.partial(per_device, dims),
            mesh=mesh,
            in_specs=placed,
            out_specs=(P("gx", "gy", None), P("gx", "gy", None), P(), P(), P(), P(), P()),
            check_vma=False,
        )(fields, w_down, w_pool, w_mid, w_unpool, w_up, cotangent)

    return whole
```

time: 231 us -> 48.4 us (0.21)
  blocking collectives: 76.1 us -> 0 us
  Pallas kernels: 0 us -> 44.2 us
  starting transfers between devices: 39.2 us -> 0 us
  matrix products: 36.7 us -> 0 us
  local copies, waits for them, and re-layouts: 33.6 us -> 3.33 us
  other arithmetic: 24.1 us -> 0 us
  waiting for transfers between devices: 17.8 us -> 0 us
    all_gather x1 -> x0, blocking collectives: 76.1 us -> none  [summed_over(): lax.all_gather(jnp.sum(pieces, axis=0) * scale, axes, axis=0, tiled=True)]
    pallas_call x0 -> x2, Pallas kernels: none -> 44.2 us  [the longest x1 41.3 us: per_device(): pl.pallas_call(functools.partial(main_kernel, dims), out_shape=(split, sp...]
    dot_general x28 -> x0, matrix products: 36.7 us -> none  [the longest x6 11.2 us: conv_padded(): jnp.dot(columns(padded), band, preferred_element_type=jnp.float32)]
    ppermute x20 -> x0, starting transfers between devices: 34.1 us -> none  [the longest x10 28 us: padded_2(): lax.ppermute(lax.slice_in_dim(block, 0, width, axis=dim), axis, backward)]
    ppermute x20 -> x0, waiting for transfers between devices: 17.8 us -> none  [the longest x10 17.6 us: padded_2(): lax.ppermute(lax.slice_in_dim(block, block.shape[dim] - width, None, axis...]
    reshape x28 -> x0, local copies, waits for them, and re-layouts: 15 us -> none  [the longest x3 5.2 us: columns(): return cols.reshape(xs * ys, -1)]
    concatenate x10 -> x0, other arithmetic: 6.2 us -> none  [padded_2(): block = jnp.concatenate([low, block, high], axis=dim)]
    select_n x4 -> x0, other arithmetic: 5.87 us -> none  [the longest x2 3.77 us: band_matrix(): band = jnp.where(offset == 1 - kk, wide[:, :, kk][:, :, None], band)]
  transfers between devices with their start and end apart: 21 -> 0, of which waited for: 5 -> 0; matrix products, arithmetic and copies ran while one was open for 29% -> 0% of each run, Pallas kernels for 0% -> 0%
where the time goes in v1:
time: 48.4 us; the launch traced here: 48.2 us
  Pallas kernels  44.2 us (91%)
  local copies, waits for them, and re-layouts  3.33 us (7%)
  between operations  0.64 us (1%)
    pallas_call x1, Pallas kernels, per_device(): pl.pallas_call(functools.partial(main_kernel, dims), out_shape=(split, sp...  41.3 us
    unnamed x2, local copies, waits for them, and re-layouts  3.33 us
    pallas_call x1, Pallas kernels, per_device(): pl.pallas_call(functools.partial(last_kernel, dims), out_shape=(flat, fla...  2.89 us

profile of v1, /device:TPU:0, one launch (start us, length us, event | category | flops | bytes accessed | tf_op | source)
XLA Modules:
  0.0 48.2 jit_solution(3101816101366056083)
XLA Ops:
  0.6 1.6 %copy.14 = bf16[2,2,2,64,32]{4,3,2,1,0:T(8,128)(2,1)} copy(bf16[2,2,2,64,32]{3,4,2,1,0:T(8,128)(2,1)} %param.11) | data formatting | bytes 65536 | tf_op args[4]
  2.2 41.3 %unet.1 = (bf16[2,256,256]{2,1,0:T(8,128)(2,1)}, bf16[2,256,256]{2,1,0:T(8,128)(2,1)}, bf16[1664,128]{1,0:T(8,128)(2,1)}) custom-call(bf16[512,256]{1,0:T(8,128)(2,1)} %bitcast.16, bf16[864,32]{1,0:T(8,128)(2,1)} %bitcast.19, bf16[256,64]{1,0:T(8,128)(2,1)} %bitcast.21, bf16[1728,64]{1,0:T(8,128)(2,1)} %bitcast.15, bf16[512,32]{1,0:T(8,128)(2,1)} %bitcast.14, ...), custom_call_target="tpu_custom_call" | custom-call | tf_op jit(solution)/shard_map/unet/pallas_call | solution.py:579
  43.5 2.9 %layouts.1 = (bf16[512,256]{1,0:T(8,128)(2,1)}, bf16[512,256]{1,0:T(8,128)(2,1)}, f32[864,32]{1,0:T(8,128)}, f32[256,64]{1,0:T(8,128)}, f32[1728,64]{1,0:T(8,128...) custom-call(bf16[2,256,256]{2,1,0:T(8,128)(2,1)} %get-tuple-element.17.out_s, bf16[2,256,256]{2,1,0:T(8,128)(2,1)} %get-tuple-element.18.gf_s, ...), custom_call_target="tpu_custom_call" | custom-call | tf_op jit(solution)/shard_map/layouts/pallas_call | solution.py:627
  46.4 1.7 %copy.15 = f32[2,2,2,64,32]{3,4,2,1,0:T(8,128)} copy(f32[2,2,2,64,32]{4,3,2,1,0:T(8,128)} %bitcast.18) | data formatting | bytes 131072

commit v2 on v1

v2 whole, which is shorter than its diff:
```python
import functools
import math

import jax
import jax.numpy as jnp
from jax import lax
from jax.experimental import pallas as pl
from jax.experimental.pallas import tpu as pltpu
from jax.sharding import PartitionSpec as P

BF16 = jnp.bfloat16
F32 = jnp.float32
MESH = pl.DeviceIdType.MESH
LANES = 128
ROWS = 16


def dot(left, right):
    return lax.dot_general(left, right, (((1,), (0,)), ((), ())), preferred_element_type=F32)


def dot_t(left, right):
    return lax.dot_general(left, right, (((1,), (1,)), ((), ())), preferred_element_type=F32)


def iota(shape, dim):
    return lax.broadcasted_iota(jnp.int32, shape, dim)


def div(value, by):
    return lax.div(value, jnp.int32(by))


def rem(value, by):
    return lax.rem(value, jnp.int32(by))


def one_hot(mask):
    return jnp.where(mask, 1.0, 0.0).astype(BF16)


def silu_parts(value):
    sig = jax.nn.sigmoid(value)
    return value * sig, sig * (1.0 + value * (1.0 - sig))


def row_matrix(xs, ys):
    hx = xs // 2
    shape = (xs * ys, xs * ys)
    row, col = iota(shape, 0), iota(shape, 1)
    place = rem(row, xs)
    across = rem(place, hx) * 2 + div(place, hx)
    return one_hot(col == across * ys + div(row, xs))


def row_matrix_back(xs, ys):
    hx = xs // 2
    shape = (xs * ys, xs * ys)
    row, col = iota(shape, 0), iota(shape, 1)
    across = div(row, ys)
    return one_hot(col == rem(row, ys) * xs + rem(across, 2) * hx + div(across, 2))


def fine_shift(lines, xs, step):
    hx = xs // 2
    shape = (lines * xs, lines * xs)
    row, col = iota(shape, 0), iota(shape, 1)
    place = rem(row, xs)
    first = place < hx
    if step > 0:
        wanted = jnp.where(first, row + hx, row - hx + 1)
        edge = xs - 1
    else:
        wanted = jnp.where(first, row + hx - 1, row - hx)
        edge = 0
    return one_hot((col == wanted) & (place != edge))


def coarse_shift(lines, hx, step):
    shape = (lines * hx, lines * hx)
    row, col = iota(shape, 0), iota(shape, 1)
    edge = hx - 1 if step > 0 else 0
    return one_hot((col == row + step) & (rem(row, hx) != edge))


def halo_matrix(lines, across, depth, base, step):
    shape = (lines * across, depth)
    row, col = iota(shape, 0), iota(shape, 1)
    edge = across - 1 if step > 0 else 0
    return one_hot((rem(row, across) == edge) & (col == div(row, across) + base))


def edge_matrix(rows, lines, across, base):
    shape = (2 * rows, lines * across)
    row, col = iota(shape, 0), iota(shape, 1)
    first = row < rows
    line = jnp.where(first, row, row - rows) - base
    return one_hot(col == line * across + jnp.where(first, 0, across - 1))


def tile_matrix(small, width):
    shape = (small, width)
    return one_hot(rem(iota(shape, 1), small) == iota(shape, 0))


def build_band(weight, band, planes, chan, width):
    tile = tile_matrix(chan, width)
    plane = div(iota((chan, width), 1), chan)

    def step(tap, carry):
        start = pl.multiple_of(tap * (3 * chan), ROWS)
        wide = dot(weight[pl.ds(start, 3 * chan), :], tile)
        spot = rem(tap, 3) * 3 + div(tap, 3)
        parts = [wide[kk * chan : (kk + 1) * chan] for kk in range(3)]
        for pp in range(planes):
            block = jnp.zeros((chan, width), F32)
            for kk in range(3):
                block = jnp.where(plane == pp + 1 - kk, parts[kk], block)
            band[spot, pp * chan : (pp + 1) * chan, :] = block.astype(BF16)
        return carry

    lax.fori_loop(0, 9, step, 0)


def build_pool(weight, mats, half, cf, cc, width):
    wide = dot(weight[...], tile_matrix(cc, width))
    plane = div(iota((2 * cf, width), 1), cc)
    for ij in range(4):
        part = wide[ij * 2 * cf : (ij + 1) * 2 * cf]
        for zz in range(half):
            block = jnp.where(plane == zz, part, 0.0)
            mats[ij, zz * 2 * cf : (zz + 1) * 2 * cf, :] = block.astype(BF16)


def folded(block, chan):
    total = block[:, :LANES]
    for part in range(1, block.shape[1] // LANES):
        total = total + block[:, part * LANES : (part + 1) * LANES]
    step = LANES // 2
    while step >= chan:
        total = total + pltpu.roll(total, step, 1)
        step //= 2
    return total


class Packer:
    def __init__(self, target, row, chan):
        self.target, self.row, self.chan = target, row, chan
        self.per = LANES // chan
        self.group = div(iota((chan, LANES), 1), chan)
        self.held, self.count = None, 0

    def add(self, value):
        spot = self.count % self.per
        self.held = value if spot == 0 else jnp.where(self.group == spot, value, self.held)
        self.count += 1
        if spot == self.per - 1:
            self.flush()

    def flush(self):
        if self.held is not None:
            self.target[self.row : self.row + self.chan, :] = self.held.astype(BF16)
            self.row += self.chan
            self.held = None
        return self.row


def conv_grad(parts, tap_of, planes, chan, width, packer, sign=1):
    plane = div(iota((chan, width), 1), chan)
    for tap in range(9):
        dband = None
        for index, part in enumerate(parts):
            term = dot(part, tap_of(index, tap // 3, tap % 3))
            dband = term if dband is None else dband + term
        for kk in range(3):
            total = jnp.zeros((chan, width), F32)
            for zz in range(planes):
                lane = zz + sign * (kk - 1)
                if 0 <= lane < planes:
                    rows = dband[zz * chan : (zz + 1) * chan]
                    total = jnp.where(plane == lane, rows, total)
            packer.add(folded(total, chan))
    return packer.flush()


def pair_grad(left_t, rights, half, chan, width, packer):
    plane = div(iota((chan, width), 1), width // half)
    for right in rights:
        full = dot(left_t, right)
        total = jnp.zeros((chan, width), F32)
        for zz in range(half):
            total = jnp.where(plane == zz, full[zz * chan : (zz + 1) * chan], total)
        packer.add(folded(total, width // half))
    return packer.flush()


def turned(value):
    return value.astype(F32).T.astype(BF16)


def turned_blocks(source, row, chan, target):
    done, total = 0, target.shape[0]
    while done < total:
        block = source[row : row + chan, :].astype(F32).T
        count = min(LANES, total - done)
        target[done : done + count, :] = block[:count]
        row, done = row + chan, done + count
    return row


PAD = 8
CPAD = 4
FAR_FIELDS, FAR_COT = 7, 5


def main_kernel(
    dims, fields_in, w_down_in, w_pool_in, w_mid_in, w_unpool_in, w_up_in, cot_in,
    out_hbm, gf_hbm, grads_hbm,
    out_s, gf_s, grads,
    raw, w_down, w_pool, w_mid, w_unpool, w_up,
    fc, sk, dd, co, dm,
    sk_send, dd_send, co_send, dm_send,
    fc_recv, sk_recv, dd_recv, co_recv, dm_recv,
    b_down, b_up, b_mid, p_mat, u_mat,
    shift, place, shift_c, place_c, order, back,
    hid, ds_down, g_skip, d_up,
    sum0, sum1, sum2, got0, got1, got2, mid0, mid1, mid2,
    in_sem, out_sem, ex_send, ex_recv, s1, r1, s2, r2, s3, r3,
):
    nx, ny, xs, ys, cf, cc, planes, scale, sizes = dims
    half, hx, hy = planes // 2, xs // 2, ys // 2
    width = planes * cf
    chunk = ROWS
    ix, iy = lax.axis_index("gx"), lax.axis_index("gy")

    def at(dx, dy):
        return {"gx": lax.rem(ix + (dx + nx), nx), "gy": lax.rem(iy + (dy + ny), ny)}

    partners = [(dx, 0) for dx in range(1, nx)] + [(0, dy) for dy in range(1, ny)]
    partners += [(dx, dy) for dx in (-1, 1) for dy in (-1, 1)]
    barrier = pltpu.get_barrier_semaphore()
    for dx, dy in partners:
        pl.semaphore_signal(barrier, inc=1, device_id=at(dx, dy), device_id_type=MESH)

    loads = {}
    for spot, (name, src, dst) in enumerate((
        ("fields", fields_in, raw.at[0]), ("cot", cot_in, raw.at[1]), ("down", w_down_in, w_down),
        ("pool", w_pool_in, w_pool), ("up", w_up_in, w_up), ("mid", w_mid_in, w_mid),
        ("unpool", w_unpool_in, w_unpool),
    )):
        loads[name] = pltpu.make_async_copy(src, dst, in_sem.at[spot])
        loads[name].start()

    def send(src, dst, ssem, rsem, dx, dy):
        copy = pltpu.make_async_remote_copy(
            src_ref=src, dst_ref=dst, send_sem=ssem, recv_sem=rsem,
            device_id=at(dx, dy), device_id_type=MESH,
        )
        copy.start()
        return copy

    def exchange(number, snd, rcv):
        ss, rs = ex_send.at[number], ex_recv.at[number]
        return [
            send(snd.at[0], rcv.at[0], ss.at[0], rs.at[0], -1, 0),
            send(snd.at[1], rcv.at[1], ss.at[1], rs.at[1], 1, 0),
        ]

    def arrive(copies):
        for copy in copies:
            copy.wait_recv()

    def lines(buf, index, first, count, start, stop):
        value = buf[index, PAD + first : PAD + first + count, :, start:stop]
        return value.reshape(count * xs, stop - start)

    def clines(buf, first, count, start, stop):
        value = buf[CPAD + first : CPAD + first + count, :, start:stop]
        return value.reshape(count * hx, stop - start).astype(BF16)

    def fine_shifts(buf, index, halo):
        for cut in range((ys + 2 * PAD) // chunk):
            span = slice(cut * chunk, (cut + 1) * chunk)
            own = buf[index, span, :, width : 2 * width].reshape(chunk * xs, width)
            both = dot(shift[...], own)
            for side, lane in ((0, 2 * width), (1, 0)):
                moved = both[side * chunk * xs : (side + 1) * chunk * xs]
                moved = moved + dot(place[side], halo(side, cut * chunk))
                buf[index, span, :, lane : lane + width] = moved.astype(BF16).reshape(
                    chunk, xs, width
                )

    def coarse_shifts(buf, rcv):
        rows = buf.shape[0]
        own = buf[:, :, width : 2 * width].reshape(rows * hx, width).astype(BF16)
        both = dot(shift_c[...], own)
        for side, lane in ((0, 2 * width), (1, 0)):
            moved = both[side * rows * hx : (side + 1) * rows * hx]
            moved = moved + dot(place_c[side], rcv[side])
            buf[:, :, lane : lane + width] = moved.reshape(rows, hx, width)

    def fine_edges(buf, snd):
        cuts = [(-2, 2, chunk - 2), (ys, 2, 0)]
        cuts += [(first, chunk, 0) for first in range(0, ys, chunk)]
        for first, count, base in cuts:
            own = lines(buf, 0, first, count, width, 2 * width)
            row = chunk + first - base
            both = dot(edge_matrix(chunk, count, xs, base), own).astype(BF16)
            for side in range(2):
                snd[side, row : row + chunk, :] = both[side * chunk : (side + 1) * chunk]

    def coarse_edges(buf, snd):
        rows, kept = buf.shape[0], snd.shape[1]
        own = buf[:, :, width : 2 * width].reshape(rows * hx, width).astype(BF16)
        both = dot(edge_matrix(kept, rows, hx, 0), own).astype(BF16)
        for side in range(2):
            snd[side] = both[side * kept : (side + 1) * kept]

    def conv(buf, index, first, count, band):
        total = None
        for bb in range(3):
            term = dot(
                lines(buf, index, first + bb - 1, count, 0, 3 * width),
                band[3 * bb : 3 * bb + 3].reshape(3 * width, width),
            )
            total = term if total is None else total + term
        return total

    def conv_t(buf, index, first, count, band):
        total = None
        for bb in range(3):
            for aa in range(3):
                left = lines(buf, index, first + bb - 1, count, aa * width, (aa + 1) * width)
                term = dot_t(left, band[3 * (2 - bb) + 2 - aa])
                total = term if total is None else total + term
        return total

    def groups(value, count, ii, jj):
        value = value.reshape(count // 2, 2, xs, width)[:, jj, ii * hx : (ii + 1) * hx]
        return value.reshape(count // 2 * hx, width).astype(BF16)

    def woven(terms, count):
        sides = [
            jnp.concatenate(
                [terms[ii][jj].reshape(count // 2, hx, width) for ii in range(2)], axis=1
            ).reshape(count // 2, 1, xs, width)
            for jj in range(2)
        ]
        return jnp.concatenate(sides, axis=1).reshape(count, xs, width)

    def frame(buf, first, count):
        return buf[PAD + first : PAD + first + count]

    order[...] = row_matrix(xs, ys)
    for buf, index, low, high in ((fc, 0, -7, ys + 7), (fc, 1, -5, ys + 5), (sk, 0, -4, ys + 4), (dd, 0, -2, ys + 2)):
        for start, stop in ((0, PAD + low), (PAD + high, buf.shape[1])):
            buf[index, start:stop, :, width : 2 * width] = jnp.zeros((stop - start, xs, width), BF16)
    for buf, low, high in ((co, -3, hy + 3), (dm, -2, hy + 2)):
        for start, stop in ((0, CPAD + low), (CPAD + high, buf.shape[0])):
            buf[start:stop, :, width : 2 * width] = jnp.zeros((stop - start, hx, width), F32)

    for index, name in ((0, "fields"), (1, "cot")):
        loads[name].wait()
        value = dot(order[...], raw[index]).astype(BF16)
        fc[index, PAD : PAD + ys, :, width : 2 * width] = value.reshape(ys, xs, width)
    pl.semaphore_wait(barrier, len(partners))
    ss, rs = ex_send.at[0], ex_recv.at[0]
    moving, spot = [], 0
    for side, dx, row in ((0, -1, 0), (1, 1, (xs - 1) * ys)):
        for dy, first, count, target in ((0, 0, ys, chunk), (-1, 0, chunk, chunk + ys),
                                         (1, ys - chunk, chunk, 0)):
            moving.append(
                send(
                    raw.at[:, row + first : row + first + count, :],
                    fc_recv.at[side, :, target : target + count, :],
                    ss.at[spot], rs.at[spot], dx, dy,
                )
            )
            spot += 1
    for index, far in ((0, FAR_FIELDS), (1, FAR_COT)):
        for dy, first, target in ((-1, 0, ys), (1, ys - far, -far)):
            moving.append(
                send(
                    fc.at[index, PAD + first : PAD + first + far, :, width : 2 * width],
                    fc.at[index, PAD + target : PAD + target + far, :, width : 2 * width],
                    ss.at[spot], rs.at[spot], 0, dy,
                )
            )
            spot += 1

    for side, step in ((0, 1), (1, -1)):
        shift[side * chunk * xs : (side + 1) * chunk * xs, :] = fine_shift(chunk, xs, step)
        place[side] = halo_matrix(chunk, xs, 2 * chunk, chunk - PAD, step)
        tall = co.shape[0] * hx
        shift_c[side * tall : (side + 1) * tall, :] = coarse_shift(co.shape[0], hx, step)
        place_c[side] = halo_matrix(co.shape[0], hx, 2 * chunk, 0, step)
    back[...] = row_matrix_back(xs, ys)
    loads["down"].wait()
    build_band(w_down, b_down, planes, cf, width)
    loads["pool"].wait()
    build_pool(w_pool, p_mat, half, cf, cc, width)
    loads["up"].wait()
    build_band(w_up, b_up, planes, cf, width)
    loads["mid"].wait()
    build_band(w_mid, b_mid, half, cc, width)

    arrive(moving)
    sends = list(moving)

    def fine_halo(rcv):
        return lambda side, cut: rcv[side, cut : cut + 2 * chunk, :]

    fine_shifts(fc, 0, lambda side, cut: fc_recv[side, 0, cut : cut + 2 * chunk, :])
    part = hy + 6
    for first in (-6, -6 + part):
        value, slope = silu_parts(conv(fc, 0, first, part, b_down))
        value = value.astype(BF16).astype(F32)
        hid[PAD + first : PAD + first + part] = value.reshape(part, xs, width)
        ds_down[PAD + first : PAD + first + part] = slope.reshape(part, xs, width)
    pre_pool = None
    for jj in range(2):
        for ii in range(2):
            term = dot(groups(frame(hid, -6, ys + 12), ys + 12, ii, jj), p_mat[2 * ii + jj])
            pre_pool = term if pre_pool is None else pre_pool + term
    coarse, ds_pool = silu_parts(pre_pool)
    coarse = coarse.astype(BF16).astype(F32)
    co[CPAD - 3 : CPAD + hy + 3, :, width : 2 * width] = coarse.reshape(hy + 6, hx, width)
    coarse_edges(co, co_send)
    moving = exchange(1, co_send, co_recv)

    loads["unpool"].wait()
    build_pool(w_unpool, u_mat, half, cf, cc, width)
    fine_shifts(fc, 1, lambda side, cut: fc_recv[side, 1, cut : cut + 2 * chunk, :])
    part = hy + 4
    for first in (-4, -4 + part):
        value = conv_t(fc, 1, first, part, b_up)
        g_skip[PAD + first : PAD + first + part] = value.reshape(part, xs, width)

    arrive(moving)
    sends += moving
    coarse_shifts(co, co_recv)
    pre_mid = None
    for bb in range(3):
        term = dot(
            clines(co, bb - 3, hy + 4, 0, 3 * width),
            b_mid[3 * bb : 3 * bb + 3].reshape(3 * width, width),
        )
        pre_mid = term if pre_mid is None else pre_mid + term
    value, ds_mid = silu_parts(pre_mid)
    own = co[CPAD - 2 : CPAD + hy + 2, :, width : 2 * width].reshape((hy + 4) * hx, width)
    middle = (own + value).astype(BF16)
    lifted = [[dot_t(middle, u_mat[2 * ii + jj]) for jj in range(2)] for ii in range(2)]
    pre_up = frame(hid, -4, ys + 8) + woven(lifted, ys + 8)
    value, slope = silu_parts(pre_up)
    sk[0, PAD - 4 : PAD + ys + 4, :, width : 2 * width] = value.astype(BF16)
    d_up[PAD - 4 : PAD + ys + 4] = (frame(g_skip, -4, ys + 8) * slope).astype(BF16).astype(F32)
    d_middle = None
    for jj in range(2):
        for ii in range(2):
            term = dot(groups(frame(d_up, -4, ys + 8), ys + 8, ii, jj), u_mat[2 * ii + jj])
            d_middle = term if d_middle is None else d_middle + term
    d_mid = (d_middle * ds_mid).astype(BF16)
    dm[CPAD - 2 : CPAD + hy + 2, :, width : 2 * width] = d_mid.astype(F32).reshape(
        hy + 4, hx, width
    )
    coarse_edges(dm, dm_send)
    moving = exchange(2, dm_send, dm_recv)
    fine_edges(sk, sk_send)
    skips = exchange(3, sk_send, sk_recv)

    class Reduction:
        def __init__(self, group, terms, got, mids, base):
            self.group, self.terms, self.got, self.mids, self.base = group, terms, got, mids, base
            self.rows = sizes[group] // nx

        def piece(self, index):
            return pl.ds(pl.multiple_of(index * self.rows, ROWS), self.rows)

        def scatter(self):
            self.copies = []
            for dx in range(1, nx):
                target = at(dx, 0)["gx"]
                self.copies.append(
                    send(
                        self.terms.at[self.piece(target), :], self.got.at[dx - 1],
                        s1.at[self.group, dx - 1], r1.at[self.group, dx - 1], dx, 0,
                    )
                )
            return self.copies

        def across(self):
            arrive(self.copies)
            total = self.terms[self.piece(ix), :].astype(F32)
            for dx in range(1, nx):
                total = total + self.got[dx - 1].astype(F32)
            self.mids[iy] = total.astype(BF16)
            self.copies = []
            for dy in range(1, ny):
                self.copies.append(
                    send(
                        self.mids.at[iy], self.mids.at[iy],
                        s2.at[self.group, dy - 1], r2.at[self.group, dy - 1], 0, dy,
                    )
                )
            return self.copies

        def gather(self):
            arrive(self.copies)
            total = self.mids[0].astype(F32)
            for yy in range(1, ny):
                total = total + self.mids[yy].astype(F32)
            start = pl.multiple_of(self.base + ix * self.rows, ROWS)
            mine = pl.ds(start, self.rows)
            grads[mine, :] = (total * scale).astype(BF16)
            self.copies = []
            for dx in range(1, nx):
                self.copies.append(
                    send(
                        grads.at[mine, :], grads.at[mine, :],
                        s3.at[self.group, dx - 1], r3.at[self.group, dx - 1], dx, 0,
                    )
                )
            return self.copies

    def padded_tail(ref, row, group):
        if row < sizes[group]:
            ref[row:, :] = jnp.zeros((sizes[group] - row, LANES), BF16)

    cuts = range(0, ys, chunk)

    def fine_tap(buf, index, cut, aa, bb):
        return lines(buf, index, cut * chunk + bb - 1, chunk, aa * width, (aa + 1) * width)

    own_mid = d_mid.astype(F32).reshape(hy + 4, hx, width)[2 : hy + 2].reshape(hy * hx, width)
    row = conv_grad(
        [turned(own_mid)],
        lambda index, aa, bb: clines(co, bb - 1, hy, aa * width, (aa + 1) * width),
        half, cc, width, Packer(sum0, 0, cc),
    )
    padded_tail(sum0, row, 0)
    red0 = Reduction(0, sum0, got0, mid0, 0)
    sends += red0.scatter()
    row = conv_grad(
        [turned(lines(sk, 0, first, chunk, width, 2 * width)) for first in cuts],
        lambda cut, aa, bb: fine_tap(fc, 1, cut, 2 - aa, 2 - bb),
        planes, cf, width, Packer(sum1, 0, cf), -1,
    )
    own_middle = middle.astype(F32).reshape(hy + 4, hx, width)[2 : hy + 2].reshape(hy * hx, width)
    row = pair_grad(
        turned(own_middle),
        [groups(frame(d_up, 0, ys), ys, ii, jj) for ii in range(2) for jj in range(2)],
        half, cc, width, Packer(sum1, row, cc),
    )
    padded_tail(sum1, row, 1)
    red1 = Reduction(1, sum1, got1, mid1, sizes[0])
    sends += red1.scatter()

    arrive(moving)
    sends += moving
    coarse_shifts(dm, dm_recv)
    total = None
    for bb in range(3):
        for aa in range(3):
            left = clines(dm, bb - 2, hy + 2, aa * width, (aa + 1) * width)
            term = dot_t(left, b_mid[3 * (2 - bb) + 2 - aa])
            total = term if total is None else total + term
    d_coarse = d_middle.reshape(hy + 4, hx, width)[1 : hy + 3].reshape((hy + 2) * hx, width)
    d_coarse = d_coarse + total
    slope = ds_pool.reshape(hy + 6, hx, width)[2 : hy + 4].reshape((hy + 2) * hx, width)
    d_pool = (d_coarse * slope).astype(BF16)
    backs = [[dot_t(d_pool, p_mat[2 * ii + jj]) for jj in range(2)] for ii in range(2)]
    d_hidden = frame(d_up, -2, ys + 4) + woven(backs, ys + 4)
    d_down = (d_hidden * frame(ds_down, -2, ys + 4)).astype(BF16)
    dd[0, PAD - 2 : PAD + ys + 2, :, width : 2 * width] = d_down

    row = conv_grad(
        [turned(lines(dd, 0, first, chunk, width, 2 * width)) for first in cuts],
        lambda cut, aa, bb: fine_tap(fc, 0, cut, aa, bb),
        planes, cf, width, Packer(sum2, 0, cf),
    )
    own_pool = d_pool.astype(F32).reshape(hy + 2, hx, width)[1 : hy + 1].reshape(hy * hx, width)
    row = pair_grad(
        turned(own_pool),
        [groups(frame(hid, 0, ys), ys, ii, jj) for ii in range(2) for jj in range(2)],
        half, cc, width, Packer(sum2, row, cc),
    )
    padded_tail(sum2, row, 2)
    red2 = Reduction(2, sum2, got2, mid2, sizes[0] + sizes[1])
    sends += red2.scatter()
    fine_edges(dd, dd_send)
    moving = exchange(4, dd_send, dd_recv)
    sends += red0.across()
    sends += red1.across()

    def finish(buf, index, rcv, value_of, target):
        fine_shifts(buf, 0, fine_halo(rcv))
        for first in cuts:
            own = lines(fc, index, first, chunk, width, 2 * width).astype(F32)
            hid[PAD + first : PAD + first + chunk] = (
                (own + value_of(first)).astype(BF16).astype(F32).reshape(chunk, xs, width)
            )
        value = frame(hid, 0, ys).reshape(ys * xs, width).astype(BF16)
        target[...] = dot(back[...], value).astype(BF16)

    arrive(skips)
    sends += skips
    finish(sk, 0, sk_recv, lambda first: conv(sk, 0, first, chunk, b_up), out_s)
    stores = []

    def store(src, dst):
        copy = pltpu.make_async_copy(src, dst, out_sem.at[len(stores)])
        copy.start()
        stores.append(copy)

    store(out_s, out_hbm)
    sends += red2.across()
    arrive(moving)
    sends += moving
    finish(dd, 1, dd_recv, lambda first: conv_t(dd, 0, first, chunk, b_down), gf_s)
    store(gf_s, gf_hbm)
    sends += red0.gather()
    sends += red1.gather()
    sends += red2.gather()
    for red in (red0, red1, red2):
        arrive(red.copies)
        rows = pl.ds(red.base, sizes[red.group])
        store(grads.at[rows, :], grads_hbm.at[rows, :])
    for copy in sends:
        copy.wait_send()
    for copy in stores:
        copy.wait()


def last_kernel(
    dims, out_in, gf_in, grads_in, output, grad_fields, g_down, g_pool, g_mid, g_unpool, g_up,
    st_out, st_gf, grads, st_down, st_pool, st_mid, st_unpool, st_up, in_sem, out_sem,
):
    nx, ny, xs, ys, cf, cc, planes, scale, sizes = dims
    loads = [
        pltpu.make_async_copy(src, dst, in_sem.at[spot])
        for spot, (src, dst) in enumerate(((grads_in, grads), (out_in, st_out), (gf_in, st_gf)))
    ]
    for load in loads:
        load.start()
    stores = []

    def store(src, dst):
        copy = pltpu.make_async_copy(src, dst, out_sem.at[len(stores)])
        copy.start()
        stores.append(copy)

    loads[0].wait()
    turned_blocks(grads, 0, cc, st_mid)
    store(st_mid, g_mid)
    loads[1].wait()
    store(st_out, output)
    loads[2].wait()
    store(st_gf, grad_fields)
    row = sizes[0]
    for block in range(st_up.shape[0] // cf):
        first = block * cf
        spot = block % (LANES // cf)
        if spot == 0:
            held = grads[row : row + cf, :].astype(F32)
            row += cf
        moved = held if spot == 0 else pltpu.roll(held, LANES - spot * cf, 1)
        st_up[first : first + cf, :] = moved[:, :cf]
    store(st_up, g_up)
    turned_blocks(grads, row, cc, st_unpool)
    store(st_unpool, g_unpool)
    row = turned_blocks(grads, sizes[0] + sizes[1], cf, st_down)
    store(st_down, g_down)
    turned_blocks(grads, row, cc, st_pool)
    store(st_pool, g_pool)
    for copy in stores:
        copy.wait()


def per_device(dims, fields, w_down, w_pool, w_mid, w_unpool, w_up, cotangent):
    nx, ny, xs, ys, cf, cc, planes, scale, sizes = dims
    hx, hy = xs // 2, ys // 2
    width = planes * cf
    hbm = pl.BlockSpec(memory_space=pl.ANY)
    tall, tall_c = ys + 2 * PAD, hy + 2 * CPAD

    def fine(lead=1):
        return pltpu.VMEM((lead, tall, xs, 3 * width), BF16)

    def coarse():
        return pltpu.VMEM((tall_c, hx, 3 * width), F32)

    def line(*shape):
        return pltpu.VMEM((2,) + shape + (width,), BF16)

    def sems(*shape):
        return pltpu.SemaphoreType.DMA(shape)

    def f32(*shape):
        return jax.ShapeDtypeStruct(shape, F32)

    def stage(values):
        return [pltpu.VMEM(value.shape, value.dtype) for value in values]

    rows = [size // nx for size in sizes]
    flat = jax.ShapeDtypeStruct((xs * ys, width), BF16)
    kept = ys + 2 * ROWS
    weights = (
        w_down.reshape(-1, cf),
        w_pool.reshape(-1, cc),
        w_mid.reshape(-1, cc),
        jnp.swapaxes(w_unpool, 3, 4).reshape(-1, cc),
        w_up.reshape(-1, cf),
    )
    total = jax.ShapeDtypeStruct((sum(sizes), LANES), BF16)
    mains = pl.pallas_call(
        functools.partial(main_kernel, dims),
        out_shape=(flat, flat, total),
        in_specs=[hbm] * 7,
        out_specs=(hbm,) * 3,
        scratch_shapes=[
            *stage((flat, flat, total)),
            pltpu.VMEM((2, xs * ys, width), BF16),
            *stage(weights),
            fine(2), fine(), fine(), coarse(), coarse(),
            line(kept), line(kept), line(2 * ROWS), line(2 * ROWS),
            line(2, kept), line(kept), line(kept), line(2 * ROWS), line(2 * ROWS),
            pltpu.VMEM((9, width, width), BF16),
            pltpu.VMEM((9, width, width), BF16),
            pltpu.VMEM((9, width, width), BF16),
            pltpu.VMEM((4, width, width), BF16),
            pltpu.VMEM((4, width, width), BF16),
            pltpu.VMEM((2 * ROWS * xs, ROWS * xs), BF16),
            pltpu.VMEM((2, ROWS * xs, 2 * ROWS), BF16),
            pltpu.VMEM((2 * tall_c * hx, tall_c * hx), BF16),
            pltpu.VMEM((2, tall_c * hx, 2 * ROWS), BF16),
            pltpu.VMEM((xs * ys, xs * ys), BF16),
            pltpu.VMEM((xs * ys, xs * ys), BF16),
            *[pltpu.VMEM((tall, xs, width), F32) for _ in range(4)],
            *[pltpu.VMEM((size, LANES), BF16) for size in sizes],
            *[pltpu.VMEM((nx - 1, row, LANES), BF16) for row in rows],
            *[pltpu.VMEM((ny, row, LANES), BF16) for row in rows],
            sems(7), sems(5),
            sems(5, 10), sems(5, 10),
            sems(3, nx - 1), sems(3, nx - 1),
            sems(3, ny - 1), sems(3, ny - 1),
            sems(3, nx - 1), sems(3, nx - 1),
        ],
        compiler_params=pltpu.CompilerParams(
            collective_id=0, has_side_effects=True, vmem_limit_bytes=60 << 20
        ),
        name="unet",
    )(fields.reshape(xs * ys, width), *weights, cotangent.reshape(xs * ys, width))

    results = (
        flat, flat, f32(27 * cf, cf), f32(8 * cf, cc), f32(27 * cc, cc), f32(8 * cf, cc),
        f32(27 * cf, cf),
    )
    output, grad_fields, g_down, g_pool, g_mid, g_unpool, g_up = pl.pallas_call(
        functools.partial(last_kernel, dims),
        out_shape=results,
        in_specs=[hbm] * 3,
        out_specs=(hbm,) * 7,
        scratch_shapes=[*stage((flat, flat, total)), *stage(results[2:]), sems(3), sems(7)],
        name="layouts",
    )(*mains)
    swapped = w_unpool.shape[:3] + (cf, cc)
    return (
        output.reshape(fields.shape),
        grad_fields.reshape(fields.shape),
        g_down.reshape(w_down.shape),
        g_pool.reshape(w_pool.shape),
        g_mid.reshape(w_mid.shape),
        jnp.swapaxes(g_unpool.reshape(swapped), 3, 4),
        g_up.reshape(w_up.shape),
    )


def solution(mesh):
    nx, ny = mesh.shape["gx"], mesh.shape["gy"]

    def whole(fields, w_down, w_pool, w_mid, w_unpool, w_up, cotangent):
        cf, cc = w_down.shape[3], w_mid.shape[3]
        xs, ys = fields.shape[0] // nx, fields.shape[1] // ny
        planes = fields.shape[2] // cf
        scale = 1.0 / math.sqrt(fields.shape[0] * fields.shape[1] * planes)

        def blocks(taps, chan):
            return -(-taps * chan // LANES) * chan

        fine_rows = blocks(27, cf)
        pair_rows = 4 * cc * 2 * cf // LANES
        unit = ROWS * nx
        sizes = tuple(
            -(-rows // unit) * unit
            for rows in (blocks(27, cc), fine_rows + pair_rows, fine_rows + pair_rows)
        )
        dims = (nx, ny, xs, ys, cf, cc, planes, scale, sizes)
        placed = (P("gx", "gy", None), P(), P(), P(), P(), P(), P("gx", "gy", None))
        return jax.shard_map(
            functools.partial(per_device, dims),
            mesh=mesh,
            in_specs=placed,
            out_specs=(P("gx", "gy", None), P("gx", "gy", None), P(), P(), P(), P(), P()),
            check_vma=False,
        )(fields, w_down, w_pool, w_mid, w_unpool, w_up, cotangent)

    return whole
```

time: 48.4 us -> 43.6 us (0.901)
  local copies, waits for them, and re-layouts: 3.33 us -> 0 us
  Pallas kernels: 44.2 us -> 42.8 us
    unnamed x2 -> x0, local copies, waits for them, and re-layouts: 3.33 us -> none
    pallas_call x2, Pallas kernels: 44.2 us -> 42.8 us  [the longest x1 40.1 us: per_device(): pl.pallas_call(functools.partial(main_kernel, dims), out_shape=(flat, fla...]
where the time goes in v2:
time: 43.6 us; the launch traced here: 43.5 us
  Pallas kernels  42.8 us (98%)
  between operations  0.64 us (1%)
    pallas_call x1, Pallas kernels, per_device(): pl.pallas_call(functools.partial(main_kernel, dims), out_shape=(flat, fla...  40.1 us
    pallas_call x1, Pallas kernels, per_device(): pl.pallas_call(functools.partial(last_kernel, dims), out_shape=results, i...  2.76 us

profile of v2, /device:TPU:0, one launch (start us, length us, event | category | flops | bytes accessed | tf_op | source)
XLA Modules:
  0.0 43.5 jit_solution(7565596968767086943)
XLA Ops:
  0.6 40.1 %unet.1 = (bf16[512,256]{1,0:T(8,128)(2,1)}, bf16[512,256]{1,0:T(8,128)(2,1)}, bf16[1664,128]{1,0:T(8,128)(2,1)}) custom-call(bf16[512,256]{1,0:T(8,128)(2,1)} %bitcast.19, bf16[864,32]{1,0:T(8,128)(2,1)} %bitcast.21, bf16[256,64]{1,0:T(8,128)(2,1)} %bitcast.23, bf16[1728,64]{1,0:T(8,128)(2,1)} %bitcast.18, bf16[256,64]{1,0:T(8,128)(2,1)} %bitcast.24, ...), custom_call_target="tpu_custom_call" | custom-call | tf_op jit(solution)/shard_map/unet/pallas_call | solution.py:715
  40.7 2.8 %layouts.1 = (bf16[512,256]{1,0:T(8,128)(2,1)}, bf16[512,256]{1,0:T(8,128)(2,1)}, f32[864,32]{1,0:T(8,128)}, f32[256,64]{1,0:T(8,128)}, f32[1728,64]{1,0:T(8,128...) custom-call(bf16[512,256]{1,0:T(8,128)(2,1)} %get-tuple-element.17.out_in, bf16[512,256]{1,0:T(8,128)(2,1)} %get-tuple-element.18.gf_in, ...), custom_call_target="tpu_custom_call" | custom-call | tf_op jit(solution)/shard_map/layouts/pallas_call | solution.py:758

commit v3 on v2

--- a/solution.py
+++ b/solution.py
@@ -28,11 +28,19 @@
 
 
 def div(value, by):
+    if by & (by - 1) == 0:
+        return lax.shift_right_logical(value, jnp.int32(by.bit_length() - 1))
     return lax.div(value, jnp.int32(by))
 
 
 def rem(value, by):
+    if by & (by - 1) == 0:
+        return value & jnp.int32(by - 1)
     return lax.rem(value, jnp.int32(by))
+
+
+def row_col(shape):
+    return iota((shape[0], 1), 0), iota((1, shape[1]), 1)
 
 
 def one_hot(mask):
@@ -47,7 +55,7 @@
 def row_matrix(xs, ys):
     hx = xs // 2
     shape = (xs * ys, xs * ys)
-    row, col = iota(shape, 0), iota(shape, 1)
+    row, col = row_col(shape)
     place = rem(row, xs)
     across = rem(place, hx) * 2 + div(place, hx)
     return one_hot(col == across * ys + div(row, xs))
@@ -56,7 +64,7 @@
 def row_matrix_back(xs, ys):
     hx = xs // 2
     shape = (xs * ys, xs * ys)
-    row, col = iota(shape, 0), iota(shape, 1)
+    row, col = row_col(shape)
     across = div(row, ys)
     return one_hot(col == rem(row, ys) * xs + rem(across, 2) * hx + div(across, 2))
 
@@ -64,7 +72,7 @@
 def fine_shift(lines, xs, step):
     hx = xs // 2
     shape = (lines * xs, lines * xs)
-    row, col = iota(shape, 0), iota(shape, 1)
+    row, col = row_col(shape)
     place = rem(row, xs)
     first = place < hx
     if step > 0:
@@ -78,21 +86,21 @@
 
 def coarse_shift(lines, hx, step):
     shape = (lines * hx, lines * hx)
-    row, col = iota(shape, 0), iota(shape, 1)
+    row, col = row_col(shape)
     edge = hx - 1 if step > 0 else 0
     return one_hot((col == row + step) & (rem(row, hx) != edge))
 
 
 def halo_matrix(lines, across, depth, base, step):
     shape = (lines * across, depth)
-    row, col = iota(shape, 0), iota(shape, 1)
+    row, col = row_col(shape)
     edge = across - 1 if step > 0 else 0
     return one_hot((rem(row, across) == edge) & (col == div(row, across) + base))
 
 
 def edge_matrix(rows, lines, across, base):
     shape = (2 * rows, lines * across)
-    row, col = iota(shape, 0), iota(shape, 1)
+    row, col = row_col(shape)
     first = row < rows
     line = jnp.where(first, row, row - rows) - base
     return one_hot(col == line * across + jnp.where(first, 0, across - 1))
@@ -100,7 +108,8 @@
 
 def tile_matrix(small, width):
     shape = (small, width)
-    return one_hot(rem(iota(shape, 1), small) == iota(shape, 0))
+    row, col = row_col(shape)
+    return one_hot(rem(col, small) == row)
 
 
 def build_band(weight, band, planes, chan, width):
@@ -210,7 +219,7 @@
 
 PAD = 8
 CPAD = 4
-FAR_FIELDS, FAR_COT = 7, 5
+FAR_FIELDS, FAR_COT = 5, 3
 
 
 def main_kernel(
@@ -266,6 +275,23 @@
             send(snd.at[1], rcv.at[1], ss.at[1], rs.at[1], 1, 0),
         ]
 
+    def around(number, snd, rcv, start):
+        ss, rs = ex_send.at[number], ex_recv.at[number]
+        copies, spot = [], 0
+        for side, dx in ((0, -1), (1, 1)):
+            for dy, first, count, target in ((0, 0, ys, chunk), (-1, 0, chunk, chunk + ys),
+                                             (1, ys - chunk, chunk, 0)):
+                if start is None:
+                    src = snd[side].at[:, first : first + count, :]
+                    dst = rcv[side].at[:, target : target + count, :]
+                else:
+                    first = first + chunk
+                    src = snd.at[side, first : first + count, :]
+                    dst = rcv.at[side, target : target + count, :]
+                copies.append(send(src, dst, ss.at[spot], rs.at[spot], dx, dy))
+                spot += 1
+        return copies
+
     def arrive(copies):
         for copy in copies:
             copy.wait_recv()
@@ -299,8 +325,8 @@
             moved = moved + dot(place_c[side], rcv[side])
             buf[:, :, lane : lane + width] = moved.reshape(rows, hx, width)
 
-    def fine_edges(buf, snd):
-        cuts = [(-2, 2, chunk - 2), (ys, 2, 0)]
+    def fine_edges(buf, snd, outer):
+        cuts = [(-2, 2, chunk - 2), (ys, 2, 0)] if outer else []
         cuts += [(first, chunk, 0) for first in range(0, ys, chunk)]
         for first, count, base in cuts:
             own = lines(buf, 0, first, count, width, 2 * width)
@@ -352,10 +378,10 @@
         return buf[PAD + first : PAD + first + count]
 
     order[...] = row_matrix(xs, ys)
-    for buf, index, low, high in ((fc, 0, -7, ys + 7), (fc, 1, -5, ys + 5), (sk, 0, -4, ys + 4), (dd, 0, -2, ys + 2)):
+    for buf, index, low, high in ((fc, 0, -5, ys + 5), (fc, 1, -3, ys + 3), (sk, 0, -2, ys + 2), (dd, 0, -1, ys + 1)):
         for start, stop in ((0, PAD + low), (PAD + high, buf.shape[1])):
             buf[index, start:stop, :, width : 2 * width] = jnp.zeros((stop - start, xs, width), BF16)
-    for buf, low, high in ((co, -3, hy + 3), (dm, -2, hy + 2)):
+    for buf, low, high in ((co, -2, hy + 2), (dm, -1, hy + 1)):
         for start, stop in ((0, CPAD + low), (CPAD + high, buf.shape[0])):
             buf[start:stop, :, width : 2 * width] = jnp.zeros((stop - start, hx, width), F32)
 
@@ -364,29 +390,23 @@
         value = dot(order[...], raw[index]).astype(BF16)
         fc[index, PAD : PAD + ys, :, width : 2 * width] = value.reshape(ys, xs, width)
     pl.semaphore_wait(barrier, len(partners))
-    ss, rs = ex_send.at[0], ex_recv.at[0]
-    moving, spot = [], 0
-    for side, dx, row in ((0, -1, 0), (1, 1, (xs - 1) * ys)):
-        for dy, first, count, target in ((0, 0, ys, chunk), (-1, 0, chunk, chunk + ys),
-                                         (1, ys - chunk, chunk, 0)):
-            moving.append(
+    rows = tuple(raw.at[:, row : row + ys, :] for row in (0, (xs - 1) * ys))
+    moving = around(0, rows, tuple(fc_recv.at[side] for side in range(2)), None)
+
+    def far_lines(index, far, spot):
+        copies = []
+        for dy, first, target in ((-1, 0, ys), (1, ys - far, -far)):
+            copies.append(
                 send(
-                    raw.at[:, row + first : row + first + count, :],
-                    fc_recv.at[side, :, target : target + count, :],
-                    ss.at[spot], rs.at[spot], dx, dy,
+                    fc.at[index, PAD + first : PAD + first + far, :, width : 2 * width],
+                    fc.at[index, PAD + target : PAD + target + far, :, width : 2 * width],
+                    ex_send.at[0, spot], ex_recv.at[0, spot], 0, dy,
                 )
             )
             spot += 1
-    for index, far in ((0, FAR_FIELDS), (1, FAR_COT)):
-        for dy, first, target in ((-1, 0, ys), (1, ys - far, -far)):
-            moving.append(
-                send(
-                    fc.at[index, PAD + first : PAD + first + far, :, width : 2 * width],
-                    fc.at[index, PAD + target : PAD + target + far, :, width : 2 * width],
-                    ss.at[spot], rs.at[spot], 0, dy,
-                )
-            )
-            spot += 1
+        return copies
+
+    moving += far_lines(0, FAR_FIELDS, 6)
 
     for side, step in ((0, 1), (1, -1)):
         shift[side * chunk * xs : (side + 1) * chunk * xs, :] = fine_shift(chunk, xs, step)
@@ -399,6 +419,7 @@
     build_band(w_down, b_down, planes, cf, width)
     loads["pool"].wait()
     build_pool(w_pool, p_mat, half, cf, cc, width)
+    far_cot = far_lines(1, FAR_COT, 8)
     loads["up"].wait()
     build_band(w_up, b_up, planes, cf, width)
     loads["mid"].wait()
@@ -411,8 +432,8 @@
         return lambda side, cut: rcv[side, cut : cut + 2 * chunk, :]
 
     fine_shifts(fc, 0, lambda side, cut: fc_recv[side, 0, cut : cut + 2 * chunk, :])
-    part = hy + 6
-    for first in (-6, -6 + part):
+    part = hy + 4
+    for first in (-4, -4 + part):
         value, slope = silu_parts(conv(fc, 0, first, part, b_down))
         value = value.astype(BF16).astype(F32)
         hid[PAD + first : PAD + first + part] = value.reshape(part, xs, width)
@@ -420,19 +441,21 @@
     pre_pool = None
     for jj in range(2):
         for ii in range(2):
-            term = dot(groups(frame(hid, -6, ys + 12), ys + 12, ii, jj), p_mat[2 * ii + jj])
+            term = dot(groups(frame(hid, -4, ys + 8), ys + 8, ii, jj), p_mat[2 * ii + jj])
             pre_pool = term if pre_pool is None else pre_pool + term
     coarse, ds_pool = silu_parts(pre_pool)
     coarse = coarse.astype(BF16).astype(F32)
-    co[CPAD - 3 : CPAD + hy + 3, :, width : 2 * width] = coarse.reshape(hy + 6, hx, width)
+    co[CPAD - 2 : CPAD + hy + 2, :, width : 2 * width] = coarse.reshape(hy + 4, hx, width)
     coarse_edges(co, co_send)
     moving = exchange(1, co_send, co_recv)
 
     loads["unpool"].wait()
     build_pool(w_unpool, u_mat, half, cf, cc, width)
+    arrive(far_cot)
+    sends += far_cot
     fine_shifts(fc, 1, lambda side, cut: fc_recv[side, 1, cut : cut + 2 * chunk, :])
-    part = hy + 4
-    for first in (-4, -4 + part):
+    part = hy + 2
+    for first in (-2, -2 + part):
         value = conv_t(fc, 1, first, part, b_up)
         g_skip[PAD + first : PAD + first + part] = value.reshape(part, xs, width)
 
@@ -442,30 +465,30 @@
     pre_mid = None
     for bb in range(3):
         term = dot(
-            clines(co, bb - 3, hy + 4, 0, 3 * width),
+            clines(co, bb - 2, hy + 2, 0, 3 * width),
             b_mid[3 * bb : 3 * bb + 3].reshape(3 * width, width),
         )
         pre_mid = term if pre_mid is None else pre_mid + term
     value, ds_mid = silu_parts(pre_mid)
-    own = co[CPAD - 2 : CPAD + hy + 2, :, width : 2 * width].reshape((hy + 4) * hx, width)
+    own = co[CPAD - 1 : CPAD + hy + 1, :, width : 2 * width].reshape((hy + 2) * hx, width)
     middle = (own + value).astype(BF16)
     lifted = [[dot_t(middle, u_mat[2 * ii + jj]) for jj in range(2)] for ii in range(2)]
-    pre_up = frame(hid, -4, ys + 8) + woven(lifted, ys + 8)
+    pre_up = frame(hid, -2, ys + 4) + woven(lifted, ys + 4)
     value, slope = silu_parts(pre_up)
-    sk[0, PAD - 4 : PAD + ys + 4, :, width : 2 * width] = value.astype(BF16)
-    d_up[PAD - 4 : PAD + ys + 4] = (frame(g_skip, -4, ys + 8) * slope).astype(BF16).astype(F32)
+    sk[0, PAD - 2 : PAD + ys + 2, :, width : 2 * width] = value.astype(BF16)
+    d_up[PAD - 2 : PAD + ys + 2] = (frame(g_skip, -2, ys + 4) * slope).astype(BF16).astype(F32)
     d_middle = None
     for jj in range(2):
         for ii in range(2):
-            term = dot(groups(frame(d_up, -4, ys + 8), ys + 8, ii, jj), u_mat[2 * ii + jj])
+            term = dot(groups(frame(d_up, -2, ys + 4), ys + 4, ii, jj), u_mat[2 * ii + jj])
             d_middle = term if d_middle is None else d_middle + term
     d_mid = (d_middle * ds_mid).astype(BF16)
-    dm[CPAD - 2 : CPAD + hy + 2, :, width : 2 * width] = d_mid.astype(F32).reshape(
-        hy + 4, hx, width
+    dm[CPAD - 1 : CPAD + hy + 1, :, width : 2 * width] = d_mid.astype(F32).reshape(
+        hy + 2, hx, width
     )
     coarse_edges(dm, dm_send)
     moving = exchange(2, dm_send, dm_recv)
-    fine_edges(sk, sk_send)
+    fine_edges(sk, sk_send, True)
     skips = exchange(3, sk_send, sk_recv)
 
     class Reduction:
@@ -531,7 +554,7 @@
     def fine_tap(buf, index, cut, aa, bb):
         return lines(buf, index, cut * chunk + bb - 1, chunk, aa * width, (aa + 1) * width)
 
-    own_mid = d_mid.astype(F32).reshape(hy + 4, hx, width)[2 : hy + 2].reshape(hy * hx, width)
+    own_mid = d_mid.astype(F32).reshape(hy + 2, hx, width)[1 : hy + 1].reshape(hy * hx, width)
     row = conv_grad(
         [turned(own_mid)],
         lambda index, aa, bb: clines(co, bb - 1, hy, aa * width, (aa + 1) * width),
@@ -545,7 +568,7 @@
         lambda cut, aa, bb: fine_tap(fc, 1, cut, 2 - aa, 2 - bb),
         planes, cf, width, Packer(sum1, 0, cf), -1,
     )
-    own_middle = middle.astype(F32).reshape(hy + 4, hx, width)[2 : hy + 2].reshape(hy * hx, width)
+    own_middle = middle.astype(F32).reshape(hy + 2, hx, width)[1 : hy + 1].reshape(hy * hx, width)
     row = pair_grad(
         turned(own_middle),
         [groups(frame(d_up, 0, ys), ys, ii, jj) for ii in range(2) for jj in range(2)],
@@ -561,35 +584,42 @@
     total = None
     for bb in range(3):
         for aa in range(3):
-            left = clines(dm, bb - 2, hy + 2, aa * width, (aa + 1) * width)
+            left = clines(dm, bb - 1, hy, aa * width, (aa + 1) * width)
             term = dot_t(left, b_mid[3 * (2 - bb) + 2 - aa])
             total = term if total is None else total + term
-    d_coarse = d_middle.reshape(hy + 4, hx, width)[1 : hy + 3].reshape((hy + 2) * hx, width)
+    d_coarse = d_middle.reshape(hy + 2, hx, width)[1 : hy + 1].reshape(hy * hx, width)
     d_coarse = d_coarse + total
-    slope = ds_pool.reshape(hy + 6, hx, width)[2 : hy + 4].reshape((hy + 2) * hx, width)
+    slope = ds_pool.reshape(hy + 4, hx, width)[2 : hy + 2].reshape(hy * hx, width)
     d_pool = (d_coarse * slope).astype(BF16)
     backs = [[dot_t(d_pool, p_mat[2 * ii + jj]) for jj in range(2)] for ii in range(2)]
-    d_hidden = frame(d_up, -2, ys + 4) + woven(backs, ys + 4)
-    d_down = (d_hidden * frame(ds_down, -2, ys + 4)).astype(BF16)
-    dd[0, PAD - 2 : PAD + ys + 2, :, width : 2 * width] = d_down
-
+    d_hidden = frame(d_up, 0, ys) + woven(backs, ys)
+    d_down = (d_hidden * frame(ds_down, 0, ys)).astype(BF16)
+    dd[0, PAD : PAD + ys, :, width : 2 * width] = d_down
+
+    sends += red0.across()
     row = conv_grad(
         [turned(lines(dd, 0, first, chunk, width, 2 * width)) for first in cuts],
         lambda cut, aa, bb: fine_tap(fc, 0, cut, aa, bb),
         planes, cf, width, Packer(sum2, 0, cf),
     )
-    own_pool = d_pool.astype(F32).reshape(hy + 2, hx, width)[1 : hy + 1].reshape(hy * hx, width)
     row = pair_grad(
-        turned(own_pool),
+        turned(d_pool),
         [groups(frame(hid, 0, ys), ys, ii, jj) for ii in range(2) for jj in range(2)],
         half, cc, width, Packer(sum2, row, cc),
     )
     padded_tail(sum2, row, 2)
     red2 = Reduction(2, sum2, got2, mid2, sizes[0] + sizes[1])
     sends += red2.scatter()
-    fine_edges(dd, dd_send)
-    moving = exchange(4, dd_send, dd_recv)
-    sends += red0.across()
+    fine_edges(dd, dd_send, False)
+    moving = around(4, dd_send, dd_recv, 0)
+    for spot, dy, first, target in ((6, -1, 0, ys), (7, 1, ys - 1, -1)):
+        moving.append(
+            send(
+                dd.at[0, PAD + first : PAD + first + 1, :, width : 2 * width],
+                dd.at[0, PAD + target : PAD + target + 1, :, width : 2 * width],
+                ex_send.at[4, spot], ex_recv.at[4, spot], 0, dy,
+            )
+        )
     sends += red1.across()
 
     def finish(buf, index, rcv, value_of, target):
@@ -614,12 +644,12 @@
 
     store(out_s, out_hbm)
     sends += red2.across()
+    sends += red0.gather()
+    sends += red1.gather()
     arrive(moving)
     sends += moving
     finish(dd, 1, dd_recv, lambda first: conv_t(dd, 0, first, chunk, b_down), gf_s)
     store(gf_s, gf_hbm)
-    sends += red0.gather()
-    sends += red1.gather()
     sends += red2.gather()
     for red in (red0, red1, red2):
         arrive(red.copies)

time: 43.6 us -> 41.2 us (0.945)
  Pallas kernels: 42.8 us -> 40.4 us
    pallas_call x1, Pallas kernels: 40.1 us -> 37.7 us  [per_device(): pl.pallas_call(functools.partial(main_kernel, dims), out_shape=(flat, fla...]
where the time goes in v3:
time: 41.2 us; the launch traced here: 41 us
  Pallas kernels  40.4 us (98%)
  between operations  0.64 us (2%)
    pallas_call x1, Pallas kernels, per_device(): pl.pallas_call(functools.partial(main_kernel, dims), out_shape=(flat, fla...  37.7 us
    pallas_call x1, Pallas kernels, per_device(): pl.pallas_call(functools.partial(last_kernel, dims), out_shape=results, i...  2.76 us

profile of v3, /device:TPU:0, one launch (start us, length us, event | category | flops | bytes accessed | tf_op | source)
XLA Modules:
  0.0 41.0 jit_solution(13588798651411779476)
XLA Ops:
  0.6 37.7 %unet.1 = (bf16[512,256]{1,0:T(8,128)(2,1)}, bf16[512,256]{1,0:T(8,128)(2,1)}, bf16[1664,128]{1,0:T(8,128)(2,1)}) custom-call(bf16[512,256]{1,0:T(8,128)(2,1)} %bitcast.19, bf16[864,32]{1,0:T(8,128)(2,1)} %bitcast.21, bf16[256,64]{1,0:T(8,128)(2,1)} %bitcast.23, bf16[1728,64]{1,0:T(8,128)(2,1)} %bitcast.18, bf16[256,64]{1,0:T(8,128)(2,1)} %bitcast.24, ...), custom_call_target="tpu_custom_call" | custom-call | tf_op jit(solution)/shard_map/unet/pallas_call | solution.py:745
  38.3 2.8 %layouts.1 = (bf16[512,256]{1,0:T(8,128)(2,1)}, bf16[512,256]{1,0:T(8,128)(2,1)}, f32[864,32]{1,0:T(8,128)}, f32[256,64]{1,0:T(8,128)}, f32[1728,64]{1,0:T(8,128...) custom-call(bf16[512,256]{1,0:T(8,128)(2,1)} %get-tuple-element.17.out_in, bf16[512,256]{1,0:T(8,128)(2,1)} %get-tuple-element.18.gf_in, ...), custom_call_target="tpu_custom_call" | custom-call | tf_op jit(solution)/shard_map/layouts/pallas_call | solution.py:788
